TPU v7x, 32 devices: a whole 2x2x4 slice. The times are simulated.
32 devices in a mesh: dp: 8 (over z, y), seq: 4 (over x, core).
Axes of the slice: x: 2, y: 2, z: 4, core: 2. Of those that a mesh axis runs over, the one named last changes fastest.
Arguments:
- byte_ids: int32 [24, 2048], P('dp', 'seq'), may hold values from 0 to 258
- lengths: int32 [24], P('dp'), may hold values from 128 to 2048, as said below
- teacher: float32 [24, 1024, 768], P('dp', 'seq'), may hold values from -6 to 6
- embed_table: bfloat16 [259, 768], P(None, ('dp', 'seq')), may hold values from -6 to 6
- conv_weight: bfloat16 [4, 768], P(None, ('dp', 'seq')), may hold values from -3 to 3
- score_weight: bfloat16 [768], P(('dp', 'seq')), may hold values from -0.625 to 0.625
- attn_gain: bfloat16 [768], P(('dp', 'seq')), may hold values from 0.5 to 1.5
- rel_bias: bfloat16 [32, 12], replicated, may hold values from -6 to 6
- query_weight: bfloat16 [768, 768], P(('dp', 'seq')), may hold values from -0.0546875 to 0.0546875
- key_weight: bfloat16 [768, 768], P(('dp', 'seq')), may hold values from -0.21875 to 0.21875
- value_weight: bfloat16 [768, 768], P(('dp', 'seq')), may hold values from -0.21875 to 0.21875
- output_weight: bfloat16 [768, 768], P(('dp', 'seq')), may hold values from -0.875 to 0.875
- ffn_gain: bfloat16 [768], P(('dp', 'seq')), may hold values from 0.5 to 1.5
- gate_weight: bfloat16 [768, 2048], P(('dp', 'seq')), may hold values from -0.21875 to 0.21875
- up_weight: bfloat16 [768, 2048], P(('dp', 'seq')), may hold values from -0.21875 to 0.21875
- down_weight: bfloat16 [2048, 768], P(('dp', 'seq')), may hold values from -0.125 to 0.125
Outputs:
- layer_out: float32 [24, 1024, 768], P('dp', 'seq')
- loss_value: float32 [], replicated
- embed_grad: float32 [259, 768], P(None, ('dp', 'seq'))
- conv_grad: float32 [4, 768], P(None, ('dp', 'seq'))
- score_grad: float32 [768], P(('dp', 'seq'))
- attn_gain_grad: float32 [768], P(('dp', 'seq'))
- bias_grad: float32 [32, 12], replicated
- query_grad: float32 [768, 768], P(('dp', 'seq'))
- key_grad: float32 [768, 768], P(('dp', 'seq'))
- value_grad: float32 [768, 768], P(('dp', 'seq'))
- output_grad: float32 [768, 768], P(('dp', 'seq'))
- ffn_gain_grad: float32 [768], P(('dp', 'seq'))
- gate_grad: float32 [768, 2048], P(('dp', 'seq'))
- up_grad: float32 [768, 2048], P(('dp', 'seq'))
- down_grad: float32 [2048, 768], P(('dp', 'seq'))
Inputs may be any that keep to these rules, and one draw needn't show every extreme that they name: `lengths`: valid bytes of each sequence; in every draw some sequence has all 2048 bytes valid.
All inputs are finite; a program needn't handle non-finite values.
Results may differ from a plain program's by a relative error of at most 0.038.
Values may be sent and summed in bfloat16 or wider, within the bound.
No kernel may reach another device: no remote copies, remote signals or barrier semaphores. Data moves between devices by JAX's collectives and lax.ppermute only.
A program may use at most 256 MiB of HBM per device.

v0:
```python
from functools import partial

import jax
import jax.numpy as jnp
from jax import lax
from jax.experimental import pallas as pl
from jax.experimental.pallas import tpu as pltpu
from jax.sharding import PartitionSpec as P

D = 768
HEADS = 12
HEAD_DIM = 64
VOCAB = 259
BUCKETS = 32
TABLE = 384
PAIRS = HEADS // 2
SIDE = 128
ONES = 16
LEFT = 20
RIGHT = 21
HALF = 128

epsilon = 1e-06
thresholds = (12, 16, 23, 32, 46, 64, 91)
masked_score = -1000000000.0
highest = lax.Precision.HIGHEST
bf16 = jnp.bfloat16
f32 = jnp.float32
both = ("dp", "seq")


def nt(a, b):
    return lax.dot_general(a, b, (((1,), (1,)), ((), ())), preferred_element_type=f32)


def nn(a, b):
    return lax.dot_general(a, b, (((1,), (0,)), ((), ())), preferred_element_type=f32)


def bucket_of(relative):
    distance = jnp.abs(relative)
    far_bucket = 8 + sum(((distance >= border).astype(jnp.int32) for border in thresholds))
    return jnp.where(relative > 0, 16, 0).astype(jnp.int32) + jnp.where(
        distance < 8, distance, far_bucket
    )


def hot_buckets(relative):
    return (bucket_of(relative)[..., None] == jnp.arange(BUCKETS, dtype=jnp.int32)).astype(f32)


def swap(value, axis, bit):
    peers = lax.axis_size(axis)
    return lax.ppermute(value, axis, [(i, i ^ bit) for i in range(peers)])


def axis_bits(axis):
    bits, bit = [], lax.axis_size(axis) // 2
    while bit:
        bits.append((axis, bit))
        bit //= 2
    return bits


def my_bit(axis, bit):
    return (lax.axis_index(axis) // bit) % 2


def gather_stage(value, axis, bit, position):
    other = swap(value, axis, bit)
    upper = my_bit(axis, bit) == 1
    return jnp.stack(
        [jnp.where(upper, other, value), jnp.where(upper, value, other)], axis=position
    )


class RowGather:
    def __init__(self, rows, order):
        self.value = rows
        self.order = list(order)
        self.places = axis_bits("dp") + axis_bits("seq")
        self.done = []
        self.got = None

    def start(self):
        if self.order:
            self.stage = self.order.pop(0)
            self.got = swap(self.value, *self.stage)

    def finish(self, *others):
        if self.got is None:
            return
        got = after(self.got, *others) if others else self.got
        self.got = None
        place = self.places.index(self.stage)
        position = sum(p < place for p in self.done)
        self.done.append(place)
        upper = my_bit(*self.stage) == 1
        self.value = jnp.stack(
            [jnp.where(upper, got, self.value), jnp.where(upper, self.value, got)],
            axis=position,
        )

    def result(self):
        self.finish()
        while self.order:
            self.start()
            self.finish()
        return self.value


def gather_order(first_axis):
    seq, dp = axis_bits("seq"), axis_bits("dp")
    if first_axis == "y":
        return dp + seq
    return dp[:-1] + seq[:-1] + dp[-1:] + seq[-1:]


def after(value, *others):
    return lax.optimization_barrier((value,) + others)[0]


def sum_order(first):
    seq, dp = axis_bits("seq")[::-1], axis_bits("dp")[::-1]
    if first == "x":
        return seq + dp
    if first == "y":
        return seq[:1] + dp[:1] + seq[1:] + dp[1:]
    return seq[:1] + dp[1:] + seq[1:] + dp[:1]


class RowSum:
    def __init__(self, total, order):
        self.parts = [total]
        self.left = axis_bits("dp") + axis_bits("seq")
        self.order = list(order)
        self.sent = self.got = None

    def start(self):
        if not self.order:
            return
        axis, bit = self.order.pop(0)
        position = self.left.index((axis, bit))
        self.left.remove((axis, bit))
        mine = my_bit(axis, bit)

        def half(value, which):
            lead, rows, cols = value.shape
            outer = lead << position
            cut = value.reshape(outer, 2, lead * rows // (2 * outer), cols)
            picked = lax.dynamic_index_in_dim(cut, which, 1, keepdims=False)
            return picked.reshape(lead, rows // 2, cols)

        send = sum(half(value, 1 - mine).astype(f32) for value in self.parts)
        self.sent = send.astype(bf16)
        self.parts = [half(value, mine) for value in self.parts]
        self.got = swap(self.sent, axis, bit)

    def finish(self, *others):
        if self.got is not None:
            self.parts.append(after(self.got, *others) if others else self.got)
            self.got = None

    def result(self):
        self.finish()
        while self.order:
            self.start()
            self.finish()
        return sum(value.astype(f32) for value in self.parts)


def after_sends(value, *sums):
    sends = [each.sent for each in sums if each.sent is not None]
    return after(value, *sends)


class SumEverywhere:
    def __init__(self, value):
        self.value = value
        self.order = axis_bits("seq")[::-1] + axis_bits("dp")[::-1]
        self.got = None

    def start(self):
        if self.order:
            self.got = swap(self.value, *self.order.pop(0))

    def finish(self, *others):
        if self.got is not None:
            self.value = self.value + (after(self.got, *others) if others else self.got)
            self.got = None

    def result(self):
        self.finish()
        while self.order:
            self.start()
            self.finish()
        return self.value


def up(x):
    return pltpu.roll(x, x.shape[0] - 1, 0)


def down(x):
    return pltpu.roll(x, 1, 0)


def triples(c, m0, m1):
    c0, c1, c2, c3 = c
    p01, p23 = c0 + c1, c2 + c3
    t0, t1, t2, t3 = down(c3) + p01, p01 + c2, c1 + p23, p23 + up(c0)
    before, after = (down(t3), t0, t1, t2), (t1, t2, t3, up(t0))
    here = (t0, t1, t2, t3)
    return tuple(
        jnp.where(m0[k], after[k], jnp.where(m1[k], here[k], before[k])) for k in range(4)
    )


def position_marks(first, rows, total_bytes):
    row = lax.broadcasted_iota(jnp.int32, (rows, 128), 0)
    live, m0, m1 = [], [], []
    for k in range(4):
        pos = first + 4 * (row - 8) + k
        live.append(((pos >= 0) & (pos < total_bytes)).astype(f32))
        shifted = (pos + 48).astype(f32)
        third = jnp.floor((shifted + 0.5) * (1.0 / 3.0))
        rest = shifted - 3.0 * third
        m0.append(rest < 0.5)
        m1.append((rest > 0.5) & (rest < 1.5))
    return live, m0, m1


def lane_chunk(i):
    return pl.ds(pl.multiple_of(i * 128, 128), 128)


def embed_bytes(ids, table, emb):
    lane = lax.broadcasted_iota(jnp.int32, (ids.shape[0], TABLE), 1)
    emb[...] = nt((ids == lane).astype(bf16), table)


def small_rows(table, small):
    lane = lax.broadcasted_iota(jnp.int32, (8, TABLE), 1)
    row = lax.broadcasted_iota(jnp.int32, (8, TABLE), 0)
    small[...] = nt((lane == row + VOCAB).astype(bf16), table)


def all_lanes(x):
    return jnp.broadcast_to(jnp.sum(x, axis=-1, keepdims=True), x.shape)


def block_probs(emb, small, conv, accs, live, m0, m1, rows):
    accs[0:4] = jnp.zeros((4, rows, 128), f32)

    def step(i, _):
        chunk = lane_chunk(i)
        w0, w1, w2, w3 = [small[k : k + 1, chunk] for k in range(4)]
        scorer = small[4:5, chunk]
        e0, e1, e2, e3 = [emb[k * rows : (k + 1) * rows, chunk] for k in range(4)]
        e3d, e0u, e1u = down(e3), up(e0), up(e1)
        c = (
            w0 * e3d + w1 * e0 + w2 * e1 + w3 * e2,
            w0 * e0 + w1 * e1 + w2 * e2 + w3 * e3,
            w0 * e1 + w1 * e2 + w2 * e3 + w3 * e0u,
            w0 * e2 + w1 * e3 + w2 * e0u + w3 * e1u,
        )
        for k in range(4):
            value = c[k] * live[k]
            conv[k, :, chunk] = value
            accs[k] += value * scorer
        return 0

    lax.fori_loop(0, D // 128, step, 0)
    score = [all_lanes(accs[k]) for k in range(4)]
    three = triples(score, m0, m1)
    p01, p23 = score[0] + score[1], score[2] + score[3]
    quad = 0.25 * (p01 + p23)
    probs = []
    for k in range(4):
        scores = (score[k], 0.5 * (p01, p01, p23, p23)[k], three[k] * (1.0 / 3.0), quad)
        top = jnp.maximum(jnp.maximum(scores[0], scores[1]), jnp.maximum(scores[2], scores[3]))
        powers = [jnp.exp(value - top) for value in scores]
        norm = 1.0 / (powers[0] + powers[1] + powers[2] + powers[3])
        probs.append([power * norm for power in powers])
    return probs


def reach(m0, m1, k, ahead):
    one = jnp.ones(m0[k].shape, f32)
    zero = jnp.zeros_like(one)
    if ahead == 0:
        return one
    if ahead == 1:
        return jnp.where(m0[k] | m1[k], one, zero)
    if ahead == 2:
        return jnp.where(m0[k], one, zero)
    if ahead == -1:
        return jnp.where(m0[k], zero, one)
    return jnp.where(m0[k] | m1[k], zero, one)


def token_weights(probs, m0, m1):
    weights = []
    for half in range(2):
        first, second = probs[2 * half], probs[2 * half + 1]
        pair = 0.5 * (first[1] + second[1])
        quad = 0.25 * (first[3] + second[3])
        row = []
        for j in range(6):
            place = 2 * half - 2 + j
            value = jnp.zeros_like(pair)
            for k, p in ((2 * half, first), (2 * half + 1, second)):
                ahead = place - k
                if abs(ahead) <= 2:
                    value += p[2] * (1.0 / 3.0) * reach(m0, m1, k, ahead)
                if ahead == 0:
                    value += p[0]
            if 0 <= place < 4:
                value += quad
            if place // 2 == half:
                value += pair
            row.append(value)
        weights.append(row)
    return weights


def places(c):
    c0, c1, c2, c3 = c
    return ((down(c2), down(c3), c0, c1, c2, c3), (c0, c1, c2, c3, up(c0), up(c1)))


def pool_kernel(first_ref, ids, table, resid, normed, emb, small, conv, accs, tokens, *, rows, total_bytes):
    first = first_ref[0]
    embed_bytes(ids[...], table[...], emb)
    small_rows(table[...], small)
    live, m0, m1 = position_marks(first, rows, total_bytes)
    probs = block_probs(emb, small, conv, accs, live, m0, m1, rows)
    weights = token_weights(probs, m0, m1)
    for half in range(2):
        for j in range(6):
            accs[6 * half + j] = 0.5 * weights[half][j]
    own = rows - 16

    def step(i, square):
        chunk = lane_chunk(i)
        around = places([conv[k, :, chunk] for k in range(4)])
        for half in range(2):
            token = accs[6 * half] * around[half][0]
            for j in range(1, 6):
                token += accs[6 * half + j] * around[half][j]
            tokens[i, pl.ds(half, own, stride=2), :] = token[8 : 8 + own]
        values = tokens[i]
        resid[:, chunk] = values
        return square + values * values

    square = lax.fori_loop(0, D // 128, step, jnp.zeros((2 * own, 128), f32))
    scale = lax.rsqrt(jnp.sum(square, axis=-1, keepdims=True) * (1.0 / D) + epsilon)
    normed[...] = (resid[...] * scale * small[5:6, :]).astype(bf16)


def pool(first, ids, table, total_bytes):
    count, wide, _ = ids.shape
    rows = wide // 4
    tokens = 2 * (rows - 16)
    return pl.pallas_call(
        partial(pool_kernel, rows=rows, total_bytes=total_bytes),
        grid=(count,),
        in_specs=[
            pl.BlockSpec(memory_space=pltpu.SMEM),
            pl.BlockSpec((None, wide, 1), lambda i: (i, 0, 0)),
            pl.BlockSpec((D, TABLE), lambda i: (0, 0)),
        ],
        out_specs=[
            pl.BlockSpec((None, tokens, D), lambda i: (i, 0, 0)),
            pl.BlockSpec((None, tokens, D), lambda i: (i, 0, 0)),
        ],
        out_shape=[
            jax.ShapeDtypeStruct((count, tokens, D), f32),
            jax.ShapeDtypeStruct((count, tokens, D), bf16),
        ],
        scratch_shapes=[
            pltpu.VMEM((wide, D), f32),
            pltpu.VMEM((8, D), f32),
            pltpu.VMEM((4, rows, D), f32),
            pltpu.VMEM((12, rows, 128), f32),
            pltpu.VMEM((D // 128, tokens, 128), f32),
        ],
        cost_estimate=pl.CostEstimate(flops=count * 3_000_000_000, bytes_accessed=4_000_000, transcendentals=0),
        name="pool",
    )(first, ids, table)


def pool_back_kernel(
    first_ref, ids, ids_row, table, grad_normed, resid, after, embed_grad, small_grad,
    emb, small, conv, accs, tokens, pulls, emb_grad, *, rows, total_bytes,
):
    first = first_ref[0]
    own = rows - 16
    chunks = D // 128

    @pl.when(pl.program_id(0) == 0)
    def _():
        embed_grad[...] = jnp.zeros_like(embed_grad)
        small_grad[...] = jnp.zeros_like(small_grad)

    embed_bytes(ids[...], table[...], emb)
    small_rows(table[...], small)
    live, m0, m1 = position_marks(first, rows, total_bytes)

    x, gn = resid[...], grad_normed[...]
    scale = lax.rsqrt(jnp.mean(x * x, axis=-1, keepdims=True) + epsilon)
    gain = small[5:6, :]
    small_grad[5:6, :] += jnp.sum(gn * x * scale, axis=0, keepdims=True)
    gg = gain * gn
    inner = jnp.mean(gg * x, axis=-1, keepdims=True)
    total = after[...] + scale * gg - x * (scale * scale * scale * inner)
    for i in range(chunks):
        tokens[i] = total[:, i * 128 : (i + 1) * 128]

    probs = block_probs(emb, small, conv, accs, live, m0, m1, rows)
    accs[0:12] = jnp.zeros((12, rows, 128), f32)
    pulls[:, 0:8, :] = jnp.zeros((2, 8, D), f32)
    pulls[:, rows - 8 : rows, :] = jnp.zeros((2, 8, D), f32)

    def dots(i, _):
        chunk = lane_chunk(i)
        around = places([conv[k, :, chunk] for k in range(4)])
        for half in range(2):
            pulls[half, 8 : 8 + own, chunk] = 0.5 * tokens[i, pl.ds(half, own, stride=2), :]
            g = pulls[half, :, chunk]
            for j in range(6):
                accs[6 * half + j] += g * around[half][j]
        return 0

    lax.fori_loop(0, chunks, dots, 0)
    pulled = []
    for half in range(2):
        at = [all_lanes(accs[6 * half + j]) for j in range(6)]
        pair = 0.5 * (at[2] + at[3])
        quad = 0.25 * (at[2] + at[3] + (at[4] + at[5] if half == 0 else at[0] + at[1]))
        for k in (2 * half, 2 * half + 1):
            middle = k - (2 * half - 2)
            three = sum(
                at[middle + ahead] * reach(m0, m1, k, ahead)
                for ahead in range(-2, 3)
                if 0 <= middle + ahead < 6
            ) * (1.0 / 3.0)
            gd = (at[middle], pair, three, quad)
            p = probs[k]
            mean = p[0] * gd[0] + p[1] * gd[1] + p[2] * gd[2] + p[3] * gd[3]
            pulled.append([p[b] * (gd[b] - mean) for b in range(4)])

    spread = triples([pulled[k][2] for k in range(4)], m0, m1)
    quad = 0.25 * (pulled[0][3] + pulled[1][3] + pulled[2][3] + pulled[3][3])
    weights = token_weights(probs, m0, m1)
    for k in range(4):
        half = k // 2
        pair = 0.5 * (pulled[2 * half][1] + pulled[2 * half + 1][1])
        accs[k] = (pulled[k][0] + pair + spread[k] * (1.0 / 3.0) + quad) * live[k]
    inside = (lax.broadcasted_iota(jnp.int32, (rows, 128), 0) >= 8) & (
        lax.broadcasted_iota(jnp.int32, (rows, 128), 0) < 8 + own
    )
    even = [jnp.where(inside, weight, 0.0) for weight in weights[0]]
    odd = [jnp.where(inside, weight, 0.0) for weight in weights[1]]
    reached = (
        (down(odd[4]), even[2], odd[0]),
        (down(odd[5]), even[3], odd[1]),
        (even[4], odd[2], up(even[0])),
        (even[5], odd[3], up(even[1])),
    )
    for k in range(4):
        for j in range(3):
            accs[4 + 3 * k + j] = reached[k][j] * live[k]

    def back(i, _):
        chunk = lane_chunk(i)
        w0, w1, w2, w3 = [small[k : k + 1, chunk] for k in range(4)]
        scorer = small[4:5, chunk]
        g0, g1 = pulls[0, :, chunk], pulls[1, :, chunk]
        g1d, g0u = down(g1), up(g0)
        e0, e1, e2, e3 = [emb[k * rows : (k + 1) * rows, chunk] for k in range(4)]
        near = ((g1d, g0, g1), (g1d, g0, g1), (g0, g1, g0u), (g0, g1, g0u))
        score = jnp.zeros((rows, 128), f32)
        gc = []
        for k in range(4):
            score += accs[k] * conv[k, :, chunk]
            value = accs[k] * scorer
            for j in range(3):
                value += accs[4 + 3 * k + j] * near[k][j]
            gc.append(value)
        small_grad[4:5, chunk] += jnp.sum(score, axis=0, keepdims=True)
        gc0, gc1, gc2, gc3 = gc
        e3d, e0u, e1u = down(e3), up(e0), up(e1)
        taps = (
            gc0 * e3d + gc1 * e0 + gc2 * e1 + gc3 * e2,
            gc0 * e0 + gc1 * e1 + gc2 * e2 + gc3 * e3,
            gc0 * e1 + gc1 * e2 + gc2 * e3 + gc3 * e0u,
            gc0 * e2 + gc1 * e3 + gc2 * e0u + gc3 * e1u,
        )
        for k in range(4):
            small_grad[k : k + 1, chunk] += jnp.sum(taps[k], axis=0, keepdims=True)
        gc3d, gc2d, gc0u = down(gc3), down(gc2), up(gc0)
        grads = (
            w0 * gc1 + w1 * gc0 + w2 * gc3d + w3 * gc2d,
            w0 * gc2 + w1 * gc1 + w2 * gc0 + w3 * gc3d,
            w0 * gc3 + w1 * gc2 + w2 * gc1 + w3 * gc0,
            w0 * gc0u + w1 * gc3 + w2 * gc2 + w3 * gc1,
        )
        for k in range(4):
            emb_grad[k * rows : (k + 1) * rows, chunk] = grads[k].astype(bf16)
        return 0

    lax.fori_loop(0, chunks, back, 0)
    row = lax.broadcasted_iota(jnp.int32, (TABLE, 4 * rows), 0)
    embed_grad[...] += nn((ids_row[...] == row).astype(bf16), emb_grad[...])


def pool_back(seq, first, ids, ids_row, table, grad_normed, resid, after_grad, total_bytes):
    _, wide, _ = ids.shape
    rows = wide // 4
    tokens = 2 * (rows - 16)
    token_spec = pl.BlockSpec((None, tokens, D), lambda i: (seq, 0, 0))
    return pl.pallas_call(
        partial(pool_back_kernel, rows=rows, total_bytes=total_bytes),
        grid=(1,),
        in_specs=[
            pl.BlockSpec(memory_space=pltpu.SMEM),
            pl.BlockSpec((None, wide, 1), lambda i: (seq, 0, 0)),
            pl.BlockSpec((None, 1, wide), lambda i: (seq, 0, 0)),
            pl.BlockSpec((D, TABLE), lambda i: (0, 0)),
            token_spec,
            token_spec,
            token_spec,
        ],
        out_specs=[
            pl.BlockSpec((TABLE, D), lambda i: (0, 0)),
            pl.BlockSpec((8, D), lambda i: (0, 0)),
        ],
        out_shape=[
            jax.ShapeDtypeStruct((TABLE, D), f32),
            jax.ShapeDtypeStruct((8, D), f32),
        ],
        scratch_shapes=[
            pltpu.VMEM((wide, D), f32),
            pltpu.VMEM((8, D), f32),
            pltpu.VMEM((4, rows, D), f32),
            pltpu.VMEM((16, rows, 128), f32),
            pltpu.VMEM((D // 128, tokens, 128), f32),
            pltpu.VMEM((2, rows, D), f32),
            pltpu.VMEM((wide, D), bf16),
        ],
        cost_estimate=pl.CostEstimate(flops=8_000_000_000, bytes_accessed=8_000_000, transcendentals=0),
        name="pool_back",
    )(first, ids, ids_row, table, grad_normed, resid, after_grad)


def prepare_kernel(
    rank_ref, lengths_ref, bias_ref, lanes_bias, tile, turned, side, diag, *, queries, keys, parts
):
    head = pl.program_id(0)
    rank = rank_ref[0]

    @pl.when(head == 0)
    def _():
        place = lax.broadcasted_iota(jnp.int32, (BUCKETS, 6 * HALF), 1)
        inside = lax.rem(place, 2 * HALF)
        offset = jnp.where(inside < HALF, inside, inside - 2 * HALF)
        relative = (place // (2 * HALF) - 1) * HALF + offset
        bucket = lax.broadcasted_iota(jnp.int32, (BUCKETS, 6 * HALF), 0)
        hot = (bucket_of(relative) == bucket).astype(bf16)
        diag[...] = lax.dot_general(
            lanes_bias[...], hot, (((0,), (0,)), ((), ())), preferred_element_type=f32
        )
        row = lax.broadcasted_iota(jnp.int32, (keys, SIDE), 0)
        lane = lax.broadcasted_iota(jnp.int32, (keys, SIDE), 1)
        at = lax.rem(rank * queries - HALF + row + keys, keys)
        far = row >= queries + 2 * HALF
        right = far & (at > rank * queries)
        left = far & (at <= rank * queries)
        fixed = jnp.where(
            right,
            lanes_bias[31:32, :].astype(f32),
            jnp.where(left, lanes_bias[15:16, :].astype(f32), 0.0),
        )
        fixed = jnp.where((lane >= ONES) & (lane < ONES + 3), 1.0, fixed)
        fixed = jnp.where((lane == LEFT) & left | (lane == RIGHT) & right, 1.0, fixed)
        for s in range(side.shape[0]):
            masked = jnp.where(2 * at < lengths_ref[s], 0.0, masked_score)
            side[s] = jnp.where(lane == 0, masked, fixed).astype(bf16)

    blocks = []
    for index in range(3):
        line = diag[pl.ds(head + 1, 1), index * 2 * HALF : (index + 1) * 2 * HALF]
        full = jnp.broadcast_to(line, (HALF, 2 * HALF))
        blocks.append(pltpu.roll(full, 0, 1, stride=1, stride_axis=0)[:, :HALF])
    turned_blocks = [block.T.astype(bf16) for block in blocks]
    blocks = [block.astype(bf16) for block in blocks]
    behind = jnp.full((HALF, HALF), bias_ref[15, head], f32).astype(bf16)
    ahead = jnp.full((HALF, HALF), bias_ref[31, head], f32).astype(bf16)
    steps = queries // HALF
    for q in range(steps):
        for n in range(steps + 2):
            apart = n - 1 - q
            wrapped = ((n == 0) & (rank == 0), (n == steps + 1) & (rank == parts - 1))
            plain = behind if apart < -1 else ahead if apart > 1 else blocks[apart + 1]
            flipped = behind if apart < -1 else ahead if apart > 1 else turned_blocks[apart + 1]
            if n == 0:
                plain = jnp.where(wrapped[0], ahead, plain)
                flipped = jnp.where(wrapped[0], ahead, flipped)
            if n == steps + 1:
                plain = jnp.where(wrapped[1], behind, plain)
                flipped = jnp.where(wrapped[1], behind, flipped)
            tile[q * HALF : (q + 1) * HALF, n * HALF : (n + 1) * HALF] = plain
            turned[n * HALF : (n + 1) * HALF, q * HALF : (q + 1) * HALF] = flipped


def prepare(rank, lengths, bias, queries, keys, parts):
    near = queries + 2 * HALF
    seqs = lengths.shape[0]
    lanes_bias = jnp.pad(bias, ((0, 0), (1, SIDE - 1 - HEADS)))
    smem = pl.BlockSpec(memory_space=pltpu.SMEM)
    return pl.pallas_call(
        partial(prepare_kernel, queries=queries, keys=keys, parts=parts),
        grid=(HEADS,),
        in_specs=[smem, smem, smem, pl.BlockSpec((BUCKETS, SIDE), lambda i: (0, 0))],
        out_specs=[
            pl.BlockSpec((None, queries, near), lambda i: (i, 0, 0)),
            pl.BlockSpec((None, near, queries), lambda i: (i, 0, 0)),
            pl.BlockSpec((seqs, keys, SIDE), lambda i: (0, 0, 0)),
        ],
        out_shape=[
            jax.ShapeDtypeStruct((HEADS, queries, near), bf16),
            jax.ShapeDtypeStruct((HEADS, near, queries), bf16),
            jax.ShapeDtypeStruct((seqs, keys, SIDE), bf16),
        ],
        scratch_shapes=[pltpu.VMEM((SIDE, 6 * HALF), f32)],
        cost_estimate=pl.CostEstimate(flops=6_000_000_000, bytes_accessed=7_000_000, transcendentals=0),
        name="prepare",
    )(rank, lengths, bias.astype(f32), lanes_bias)


def row_offset(rank, step, blocks):
    half = lax.rem(2 * rank - 1 + step + 2 * blocks, 2 * blocks)
    apart = jnp.bitwise_xor(rank, half // 2)
    slot = (apart % 2) * 2 + apart // 2
    return pl.multiple_of(slot * (2 * HALF) + (half % 2) * HALF, HALF)


def side_lanes(rows, picks):
    lane = lax.broadcasted_iota(jnp.int32, (rows, SIDE), 1)
    value = jnp.zeros((rows, SIDE), f32)
    for index, entry in picks:
        value = jnp.where(lane == index, entry, value)
    return value.astype(bf16)


def three_parts(value):
    high = value.astype(bf16).astype(f32)
    rest = value - high
    middle = rest.astype(bf16).astype(f32)
    return high, middle, rest - middle


def one_head(values, head):
    lane = lax.broadcasted_iota(jnp.int32, values.shape, 1)
    return jnp.where((lane // HEAD_DIM) == head, values, jnp.zeros_like(values))


def attend_kernel(rank_ref, q, k, v, side, bias, out, norm, kcat, vcat, *, near, blocks):
    rank = rank_ref[0]
    pair = pl.program_id(1)
    queries = q.shape[0]

    @pl.when(pair == 0)
    def _():
        kcat[:, SIDE:] = side[...]
        vcat[:, SIDE:] = side[...]
        norm[...] = jnp.zeros_like(norm)

    for step in range(2 * blocks):
        source = pl.ds(row_offset(rank, step, blocks), HALF)
        kcat[step * HALF : (step + 1) * HALF, :SIDE] = k[source, :]
        vcat[step * HALF : (step + 1) * HALF, :SIDE] = v[source, :]

    lane = lax.broadcasted_iota(jnp.int32, (queries, SIDE), 1)
    halves = []
    for head in range(2):
        index = 2 * pair + head
        extra = side_lanes(queries, [(0, 1.0), (1 + index, 1.0)])
        wide = jnp.concatenate([one_head(q[...], head), extra], axis=1)
        logits = nt(wide, kcat[...])
        close = logits[:, :near] + bias[head].astype(f32)
        away = logits[:, near:]
        top = jnp.maximum(
            jnp.max(close, axis=-1, keepdims=True), jnp.max(away, axis=-1, keepdims=True)
        )
        close = jnp.exp(close - top).astype(bf16)
        away = jnp.exp(away - top).astype(bf16)
        mixed = nn(close, vcat[:near, :]) + nn(away, vcat[near:, :])
        total = mixed[:, SIDE + ONES : SIDE + ONES + 1]
        halves.append(mixed[:, :SIDE] * (1.0 / total))
        norm[...] = jnp.where(lane == index, top + jnp.log(total), norm[...])
    out[...] = jnp.where(lane < HEAD_DIM, halves[0], halves[1]).astype(bf16)


def attend(rank, q, kv, side, bias):
    seqs, queries, _ = q.shape
    keys = kv.shape[1]
    near = bias.shape[-1]
    blocks = keys // queries
    return pl.pallas_call(
        partial(attend_kernel, near=near, blocks=blocks),
        grid=(seqs, PAIRS),
        in_specs=[
            pl.BlockSpec(memory_space=pltpu.SMEM),
            pl.BlockSpec((None, queries, SIDE), lambda s, i: (s, 0, i)),
            pl.BlockSpec((None, keys, SIDE), lambda s, i: (s, 0, i)),
            pl.BlockSpec((None, keys, SIDE), lambda s, i: (s, 0, i + PAIRS)),
            pl.BlockSpec((None, keys, SIDE), lambda s, i: (s, 0, 0)),
            pl.BlockSpec((2, queries, near), lambda s, i: (i, 0, 0)),
        ],
        out_specs=[
            pl.BlockSpec((None, queries, SIDE), lambda s, i: (s, 0, i)),
            pl.BlockSpec((None, queries, SIDE), lambda s, i: (s, 0, 0)),
        ],
        out_shape=[
            jax.ShapeDtypeStruct((seqs, queries, D), bf16),
            jax.ShapeDtypeStruct((seqs, queries, SIDE), f32),
        ],
        scratch_shapes=[pltpu.VMEM((keys, 2 * SIDE), bf16)] * 2,
        cost_estimate=pl.CostEstimate(flops=25_000_000_000, bytes_accessed=8_000_000, transcendentals=0),
        name="attend",
    )(rank, q, kv, kv, side, bias)


def attend_back_kernel(
    rank_ref, q, k, v, side, bias, norm, mixed, grad, *rest, near, blocks, part,
):
    dq, dk, dv, dnear, dfar, kcat, vcat, kturn = rest[-8:]
    rank = rank_ref[0]
    pair = pl.program_id(0)
    queries = q.shape[0]
    keys = k.shape[0]

    @pl.when(pair == 0)
    def _():
        kcat[:, SIDE:] = side[...]
        vcat[:, SIDE:] = side[...]
        kturn[SIDE:, :] = side[...].astype(f32).T[ONES : 2 * ONES, :].astype(bf16)

    for step in range(2 * blocks):
        source = pl.ds(row_offset(rank, step, blocks), HALF)
        kcat[step * HALF : (step + 1) * HALF, :SIDE] = k[source, :]
        vcat[step * HALF : (step + 1) * HALF, :SIDE] = v[source, :]
    kturn[:SIDE, :] = kcat[:, :SIDE].astype(f32).T.astype(bf16)

    lane = lax.broadcasted_iota(jnp.int32, (queries, SIDE), 1)
    queries_of, grads_of, wide_q, wide_g = [], [], [], []
    products = grad[...].astype(f32) * mixed[...].astype(f32)
    for head in range(2):
        index = 2 * pair + head
        level = jnp.sum(jnp.where(lane == index, norm[...], 0.0), axis=-1, keepdims=True)
        delta = jnp.sum(
            jnp.where((lane // HEAD_DIM) == head, products, 0.0), axis=-1, keepdims=True
        )
        la, lb, lc = three_parts(-level)
        da, db, dc = three_parts(-delta)
        queries_of.append(one_head(q[...], head))
        grads_of.append(one_head(grad[...], head))
        extra = [(0, 1.0), (1 + index, 1.0), (ONES, la), (ONES + 1, lb), (ONES + 2, lc)]
        wide_q.append(jnp.concatenate([queries_of[head], side_lanes(queries, extra)], axis=1))
        extra = [(ONES, da), (ONES + 1, db), (ONES + 2, dc)]
        wide_g.append(jnp.concatenate([grads_of[head], side_lanes(queries, extra)], axis=1))

    sums = [jnp.zeros((kturn.shape[0], queries), f32) for _ in range(2)]
    for base in range(0, keys, part):
        span = slice(base, base + part)
        value_part = jnp.zeros((part, SIDE), f32)
        key_part = jnp.zeros((part, SIDE), f32)
        for head in range(2):
            logits = nt(kcat[span, :], wide_q[head])
            if base < near:
                logits = logits + bias[head, span, :].astype(f32)
            probs = jnp.exp(logits)
            pull = nt(vcat[span, :], wide_g[head])
            low = (probs * pull).astype(bf16)
            value_part += nn(probs.astype(bf16), grads_of[head])
            key_part += nn(low, queries_of[head])
            sums[head] += nn(kturn[:, span], low)
            if base < near:
                dnear[head, span, :] = low
        for step in range(base // HALF, (base + part) // HALF):
            target = pl.ds(row_offset(rank, step, blocks), HALF)
            inner = slice(step * HALF - base, (step + 1) * HALF - base)
            dk[target, :] = key_part[inner].astype(bf16)
            dv[target, :] = value_part[inner].astype(bf16)
    turned = jnp.concatenate([sums[0][:HEAD_DIM], sums[1][HEAD_DIM:SIDE]], axis=0)
    dq[...] = turned.T.astype(bf16)
    for head in range(2):
        dfar[head] = sums[head][SIDE:, :]


def attend_back(seq, rank, q, kv, side, bias, norm, mixed, grad, earlier):
    seqs, queries, _ = q.shape
    keys = kv.shape[1]
    near = bias.shape[1]
    blocks = keys // queries
    own = pl.BlockSpec((None, queries, SIDE), lambda i: (seq, 0, i))
    every = pl.BlockSpec((None, keys, SIDE), lambda i: (seq, 0, i))
    return pl.pallas_call(
        partial(attend_back_kernel, near=near, blocks=blocks, part=2 * HALF),
        grid=(PAIRS,),
        in_specs=[
            pl.BlockSpec(memory_space=pltpu.SMEM),
            own,
            every,
            pl.BlockSpec((None, keys, SIDE), lambda i: (seq, 0, i + PAIRS)),
            pl.BlockSpec((None, keys, SIDE), lambda i: (seq, 0, 0)),
            pl.BlockSpec((2, near, queries), lambda i: (i, 0, 0)),
            pl.BlockSpec((None, queries, SIDE), lambda i: (seq, 0, 0)),
            own,
            own,
        ]
        + [pl.BlockSpec(memory_space=pl.ANY)] * len(earlier),
        out_specs=[
            own,
            every,
            every,
            pl.BlockSpec((None, 2, near, queries), lambda i: (seq, i, 0, 0)),
            pl.BlockSpec((None, 2, ONES, queries), lambda i: (seq, i, 0, 0)),
        ],
        out_shape=[
            jax.ShapeDtypeStruct((seqs, queries, D), bf16),
            jax.ShapeDtypeStruct((seqs, keys, D), bf16),
            jax.ShapeDtypeStruct((seqs, keys, D), bf16),
            jax.ShapeDtypeStruct((seqs, HEADS, near, queries), bf16),
            jax.ShapeDtypeStruct((seqs, HEADS, ONES, queries), f32),
        ],
        scratch_shapes=[
            pltpu.VMEM((keys, 2 * SIDE), bf16),
            pltpu.VMEM((keys, 2 * SIDE), bf16),
            pltpu.VMEM((SIDE + ONES, keys), bf16),
        ],
        input_output_aliases={9 + i: i for i in range(len(earlier))},
        cost_estimate=pl.CostEstimate(flops=15_000_000_000, bytes_accessed=12_000_000, transcendentals=0),
        name="attend_back",
    )(rank, q, kv, kv, side, bias, norm, mixed, grad, *earlier)


def bias_grad_kernel(rank_ref, near, far, out, hot, *, parts):
    rank = rank_ref[0]
    seqs = near.shape[0]
    steps = near.shape[1] // HALF - 2

    @pl.when(pl.program_id(0) == 0)
    def _():
        place = lax.broadcasted_iota(jnp.int32, hot.shape, 0)
        lane = lax.broadcasted_iota(jnp.int32, hot.shape, 1)
        segment = place // (2 * HALF)
        relative = (segment - 1) * HALF + HALF - 1 - lax.rem(place, 2 * HALF)
        bucket = jnp.where(segment == 3, 15, jnp.where(segment == 4, 31, bucket_of(relative)))
        hot[...] = (bucket == lane).astype(bf16)

    row = lax.broadcasted_iota(jnp.int32, (HALF, HALF), 0)
    lane = lax.broadcasted_iota(jnp.int32, (HALF, HALF), 1)
    flip = (row + lane == HALF - 1).astype(bf16)
    ones = jnp.ones((8, HALF), bf16)
    first_in, last_in = rank != 0, rank != parts - 1

    def block(s, n, q):
        return near[s, n * HALF : (n + 1) * HALF, q * HALF : (q + 1) * HALF]

    sums = [jnp.zeros((HALF, HALF), f32) for _ in range(3)]
    left = [far[s, LEFT - ONES : LEFT - ONES + 1, :] for s in range(seqs)]
    right = [far[s, RIGHT - ONES : RIGHT - ONES + 1, :] for s in range(seqs)]
    left, right = sum(left), sum(right)
    for n in range(steps + 2):
        inside = first_in if n == 0 else last_in if n == steps + 1 else None
        tails = []
        for q in range(steps):
            apart = n - 1 - q
            if abs(apart) <= 1:
                value = sum(nn(flip, block(s, n, q)) for s in range(seqs))
                if inside is not None:
                    value = jnp.where(inside, value, 0.0)
                sums[apart + 1] += value
        if inside is not None:
            span = slice(n * HALF, (n + 1) * HALF)
            column = sum(nn(ones, near[s, span, :]) for s in range(seqs))[:1]
            at = lax.broadcasted_iota(jnp.int32, column.shape, 1) // HALF
            outside = (n - 1 - at < -1) | (n - 1 - at > 1)
            kept = jnp.where(outside, column, 0.0)
            if n == 0:
                left += jnp.where(inside, kept, 0.0)
                right += jnp.where(inside, 0.0, column)
            else:
                right += jnp.where(inside, kept, 0.0)
                left += jnp.where(inside, 0.0, column)
    lines = []
    for value in sums:
        wide = jnp.concatenate([value, jnp.zeros((HALF, HALF), f32)], axis=1)
        rolled = pltpu.roll(wide, 0, 1, stride=1, stride_axis=0)
        lines.append(jnp.sum(rolled, axis=0, keepdims=True))
    line = jnp.concatenate(lines + [left, right], axis=1)
    line = jnp.broadcast_to(line, (8, line.shape[1]))
    total = sum(nn(part.astype(bf16), hot[...]) for part in three_parts(line))
    out[...] = total[:1]


def bias_sums(rank, near_parts, far_parts, parts):
    seqs, heads, near, queries = near_parts.shape
    return pl.pallas_call(
        partial(bias_grad_kernel, parts=parts),
        grid=(heads,),
        in_specs=[
            pl.BlockSpec(memory_space=pltpu.SMEM),
            pl.BlockSpec((seqs, None, near, queries), lambda i: (0, i, 0, 0)),
            pl.BlockSpec((seqs, None, ONES, queries), lambda i: (0, i, 0, 0)),
        ],
        out_specs=pl.BlockSpec((None, 1, 128), lambda i: (i, 0, 0)),
        out_shape=jax.ShapeDtypeStruct((heads, 1, 128), f32),
        scratch_shapes=[pltpu.VMEM((10 * HALF, 128), bf16)],
        cost_estimate=pl.CostEstimate(flops=6_000_000_000, bytes_accessed=9_000_000, transcendentals=0),
        name="bias_sums",
    )(rank, near_parts, far_parts)


def gelu_parts(x):
    inner = 0.7978845608028654 * (x + 0.044715 * (x * x * x))
    t = jnp.tanh(inner)
    half = 0.5 * (1.0 + t)
    slope = half + 0.5 * x * (1.0 - t * t) * (
        0.7978845608028654 * (1.0 + 0.134145 * (x * x))
    )
    return x * half, slope


def feed_kernel(
    place_ref, count_ref, lengths_ref, att, resid, teacher, gain, gate_w, up_w, down_w, output_w,
    block_out, normed, hidden, branch, gate_low, up_low, after_grad, after_low, att_grad, stats,
    act, steep, *, chunk,
):
    step = pl.program_id(0)
    rows = att.shape[0]
    ffn_dim = gate_w.shape[1]

    @pl.when(step == 0)
    def _():
        stats[...] = jnp.zeros_like(stats)

    after = resid[...] + nn(att[...], output_w[...])
    scale = lax.rsqrt(jnp.mean(after * after, axis=-1, keepdims=True) + epsilon)
    normed[...] = (after * scale * gain[...]).astype(bf16)
    out = after
    for base in range(0, ffn_dim, chunk):
        span = slice(base, base + chunk)
        gate = nn(normed[...], gate_w[:, span])
        up_part = nn(normed[...], up_w[:, span])
        value, slope = gelu_parts(gate)
        act[:, span] = value
        steep[:, span] = slope * up_part
        low = (value * up_part).astype(bf16)
        hidden[:, span] = low
        out = out + nn(low, down_w[span, :])
    block_out[...] = out
    token = place_ref[0] + lax.broadcasted_iota(jnp.int32, (rows, D), 0)
    live = (2 * token < lengths_ref[step]).astype(f32)
    error = live * (out - teacher[...])
    stats[1:2, :] += jnp.sum(error * error, axis=0, keepdims=True)
    out_grad = (2.0 / count_ref[0]) * error
    branch[...] = out_grad.astype(bf16)
    back = jnp.zeros((rows, D), f32)
    for base in range(0, ffn_dim, chunk):
        span = slice(base, base + chunk)
        pull = nt(branch[...], down_w[span, :])
        gate_part = (pull * steep[:, span]).astype(bf16)
        up_part = (pull * act[:, span]).astype(bf16)
        gate_low[:, span] = gate_part
        up_low[:, span] = up_part
        back = back + nt(gate_part, gate_w[:, span]) + nt(up_part, up_w[:, span])
    stats[0:1, :] += jnp.sum(back * after * scale, axis=0, keepdims=True)
    gained = back * gain[...]
    inner = jnp.mean(gained * after, axis=-1, keepdims=True)
    total = out_grad + scale * gained - after * (scale * scale * scale * inner)
    after_grad[...] = total
    low = total.astype(bf16)
    after_low[...] = low
    att_grad[...] = nt(low, output_w[...]).astype(bf16)


def feed(place, count, lengths, att, resid, teacher, gain, wide, down_w):
    tokens = att.shape[0]
    seqs = lengths.shape[0]
    rows = tokens // seqs
    ffn_dim = down_w.shape[0]
    once = pl.Buffered(1)
    own = pl.BlockSpec((rows, D), lambda i: (i, 0))
    broad = pl.BlockSpec((rows, ffn_dim), lambda i: (i, 0))
    smem = pl.BlockSpec(memory_space=pltpu.SMEM)
    return pl.pallas_call(
        partial(feed_kernel, chunk=512),
        grid=(seqs,),
        in_specs=[
            smem,
            smem,
            smem,
            own,
            pl.BlockSpec((None, rows, D), lambda i: (i, 0, 0)),
            own,
            pl.BlockSpec((1, D), lambda i: (0, 0)),
            pl.BlockSpec((D, ffn_dim), lambda i: (0, 0), pipeline_mode=once),
            pl.BlockSpec((D, ffn_dim), lambda i: (0, 1), pipeline_mode=once),
            pl.BlockSpec((ffn_dim, D), lambda i: (0, 0), pipeline_mode=once),
            pl.BlockSpec((D, D), lambda i: (0, 3 * ffn_dim // D), pipeline_mode=once),
        ],
        out_specs=[own, own, broad, own, broad, broad, own, own, own, pl.BlockSpec((8, D), lambda i: (0, 0))],
        out_shape=[
            jax.ShapeDtypeStruct((tokens, D), f32),
            jax.ShapeDtypeStruct((tokens, D), bf16),
            jax.ShapeDtypeStruct((tokens, ffn_dim), bf16),
            jax.ShapeDtypeStruct((tokens, D), bf16),
            jax.ShapeDtypeStruct((tokens, ffn_dim), bf16),
            jax.ShapeDtypeStruct((tokens, ffn_dim), bf16),
            jax.ShapeDtypeStruct((tokens, D), f32),
            jax.ShapeDtypeStruct((tokens, D), bf16),
            jax.ShapeDtypeStruct((tokens, D), bf16),
            jax.ShapeDtypeStruct((8, D), f32),
        ],
        scratch_shapes=[pltpu.VMEM((rows, ffn_dim), f32)] * 2,
        cost_estimate=pl.CostEstimate(flops=17_000_000_000, bytes_accessed=30_000_000, transcendentals=0),
        name="feed",
    )(place, count, lengths, att, resid, teacher, gain, wide, wide, down_w, wide)


def dot(a, b):
    return jnp.dot(a, b, preferred_element_type=f32)


def per_device(
    byte_ids,
    lengths,
    teacher,
    embed_table,
    conv_weight,
    score_weight,
    attn_gain,
    rel_bias,
    query_weight,
    key_weight,
    value_weight,
    output_weight,
    ffn_gain,
    gate_weight,
    up_weight,
    down_weight,
):
    seqs, own_bytes = byte_ids.shape
    own = own_bytes // 2
    parts = lax.axis_size("seq")
    dp_size = lax.axis_size("dp")
    rank = lax.axis_index("seq")
    total_tokens, total_bytes = own * parts, own_bytes * parts
    shard = score_weight.shape[0]
    rank_ref = rank.reshape(1).astype(jnp.int32)

    live_here = jnp.sum(jnp.minimum((lengths + 1) // 2, total_tokens))
    live_here = jnp.where(rank == 0, live_here, 0)
    counts = jnp.stack([live_here // 64, live_here % 64])
    at_count = (jnp.arange(shard) == 0).astype(jnp.int32)
    columns = jnp.concatenate(
        [
            embed_table,
            conv_weight,
            score_weight[None],
            attn_gain[None],
            ffn_gain[None],
            (counts[:, None] * at_count[None]).astype(bf16),
            jnp.zeros((TABLE - VOCAB - 9, shard), bf16),
        ],
        axis=0,
    ).T
    ids_low = jnp.stack([byte_ids // 16, byte_ids % 16]).astype(bf16)
    id_rows = ids_low.reshape(-1, TABLE)
    attn_rows = jnp.concatenate([query_weight, key_weight, value_weight], axis=1)
    cut = attn_rows.shape[1] // 2
    qkv_halves = [
        RowGather(attn_rows[:, :cut], gather_order("y")),
        RowGather(attn_rows[:, cut:], gather_order("x")),
    ]
    small = RowGather(columns, axis_bits("dp"))
    while small.order:
        small.start()
        for each in qkv_halves:
            each.finish()
            if len(each.order) > 3:
                each.start()
        small.finish()
    value = small.value.reshape(-1, TABLE)
    mine = jnp.concatenate([value, id_rows], axis=0)
    x_other = swap(mine, "seq", 2)
    pair = jnp.concatenate([mine, x_other], axis=0)
    c_other = swap(pair, "seq", 1)
    wide_rows = mine.shape[0]
    quarters = jnp.concatenate([pair, c_other], axis=0).reshape(parts, wide_rows, TABLE)
    apart = jnp.bitwise_xor(rank, jnp.arange(parts))
    slots = (apart % 2) * 2 + apart // 2
    ordered = jnp.take(quarters, slots, axis=0)
    table = (
        ordered[:, : dp_size * shard]
        .reshape(parts, dp_size, shard, TABLE)
        .transpose(1, 0, 2, 3)
        .reshape(D, TABLE)
    )
    all_ids = ordered[:, dp_size * shard :].reshape(parts, 2, seqs, own_bytes).astype(jnp.int32)
    all_ids = (all_ids[:, 0] * 16 + all_ids[:, 1]).transpose(1, 0, 2).reshape(seqs, total_bytes)
    counts = jnp.sum(table[:, VOCAB + 7 : VOCAB + 9].astype(f32), axis=0)
    live_count = counts[0] * 64.0 + counts[1]
    ffn_gain_full = table[:, VOCAB + 6].astype(f32)

    padded_ids = jnp.pad(all_ids, ((0, 0), (32, 32)), constant_values=-1)
    first_byte = (rank * own_bytes).astype(jnp.int32)
    first_other = (jnp.bitwise_xor(rank, 2) * own_bytes).astype(jnp.int32)

    def phases(start):
        window = lax.dynamic_slice_in_dim(padded_ids, start, own_bytes + 64, 1)
        return window.reshape(seqs, -1, 4).transpose(0, 2, 1).reshape(seqs, -1)

    phase_ids = phases(first_byte)
    other_ids = phases(first_other)

    ffn_dim = gate_weight.shape[1]
    tiled = down_weight.shape[0] % 64 == 0
    third = D // 3
    if tiled:
        down_packed = down_weight.reshape(-1, 8, 8, 3, third).transpose(0, 3, 2, 1, 4)
    else:
        down_packed = down_weight
    down_packed = down_packed.reshape(shard, ffn_dim)
    packed = jnp.concatenate([gate_weight, up_weight, down_packed, output_weight], axis=1)
    wide_full = lax.all_gather(packed, both, axis=0, tiled=True)
    down_full = wide_full[:, 2 * ffn_dim : 3 * ffn_dim]
    if tiled:
        down_full = down_full.reshape(-1, 3, 8, 8, third).transpose(0, 3, 2, 1, 4)
    down_full = down_full.reshape(ffn_dim, D)

    for each in qkv_halves:
        each.start()
    residual, normed_own = pool(first_byte.reshape(1), phase_ids[:, :, None], table, total_bytes)
    for each in qkv_halves:
        each.finish(normed_own)
        each.start()
    other_first = after(first_other.reshape(1), normed_own)
    _, normed_x = pool(other_first, other_ids[:, :, None], table, total_bytes)
    normed_two = jnp.concatenate([normed_own, normed_x], axis=1)
    normed_other = swap(normed_two, "seq", 1)
    tile, turned_tile, side = prepare(
        after(rank_ref, normed_x), lengths, rel_bias, own, total_tokens, parts
    )
    for each in qkv_halves:
        each.finish(tile)
        each.start()
        each.finish()
    qkv_full = jnp.concatenate(
        [each.result().reshape(D, cut) for each in qkv_halves], axis=1
    )
    query_full, kv_full = qkv_full[:, :D], qkv_full[:, D:]
    key_full, value_full = qkv_full[:, D : 2 * D], qkv_full[:, 2 * D :]
    normed = jnp.concatenate([normed_two, normed_other], axis=1)
    own_rows = normed_own.reshape(-1, D)
    queries = dot(own_rows, query_full).astype(bf16).reshape(seqs, own, D)
    pairs_kv = dot(normed.reshape(-1, D), kv_full).astype(bf16).reshape(seqs, total_tokens, 2 * D)
    attended, norms = attend(rank_ref, queries, pairs_kv, side, tile)

    token_rows = seqs * own
    att = attended.reshape(token_rows, D)
    (
        block_out, ffn_in, hidden, branch_grad, gate_low, up_low, after_grad, after_low,
        attended_grad, feed_stats,
    ) = feed(
        (rank * own).reshape(1), live_count.reshape(1), lengths, att,
        residual, teacher.reshape(token_rows, D), ffn_gain_full[None],
        wide_full, down_full,
    )
    down_grad = jnp.einsum("tf,td->fd", hidden, branch_grad, preferred_element_type=f32)
    gate_grad = jnp.einsum("td,tf->df", ffn_in, gate_low, preferred_element_type=f32)
    up_grad = jnp.einsum("td,tf->df", ffn_in, up_low, preferred_element_type=f32)
    output_grad = jnp.einsum("td,te->de", att, after_low, preferred_element_type=f32).astype(bf16)
    down_sum = RowSum(down_grad.astype(bf16)[None], sum_order("z"))
    gate_sum = RowSum(gate_grad.astype(bf16)[None], sum_order("x"))
    up_sum = RowSum(up_grad.astype(bf16)[None], sum_order("y"))
    feed_sums = (down_sum, gate_sum, up_sum)
    for each in feed_sums:
        each.start()
    turn = after_sends(after(attended_grad, output_grad), *feed_sums).reshape(seqs, own, D)

    made = ()
    for s in range(seqs):
        made = attend_back(
            s, rank_ref, queries, pairs_kv, side, turned_tile, norms, attended, turn, made
        )
        for each in feed_sums:
            each.finish(made[4])
            each.start()
        if s < seqs - 1:
            turn = after_sends(turn, *feed_sums)
    dq, dk, dv, near_parts, far_parts = made
    dk_rows, dv_rows = dk.reshape(-1, D), dv.reshape(-1, D)
    dk_rows = after_sends(dk_rows, *feed_sums)
    pulled = (
        jnp.einsum("te,de->td", dk_rows, key_full, preferred_element_type=f32)
        + jnp.einsum("te,de->td", dv_rows, value_full, preferred_element_type=f32)
    ).reshape(seqs, total_tokens, D)
    direct = jnp.einsum(
        "te,de->td", dq.reshape(-1, D), query_full, preferred_element_type=f32
    ).reshape(seqs, own, D)
    from_core = swap(pulled[:, 2 * own :].astype(bf16), "seq", 1)
    normed_rows = normed.reshape(-1, D)
    key_grad = jnp.einsum(
        "td,te->de", normed_rows, after(dk_rows, pulled), preferred_element_type=f32
    ).astype(bf16)
    from_core = after(from_core, key_grad)
    chip = pulled[:, : 2 * own] + from_core.astype(f32)
    from_x = swap(chip[:, own:].astype(bf16), "seq", 2)
    for each in feed_sums:
        each.finish(key_grad)
        each.start()
    dv_rows = after_sends(after(dv_rows, chip), *feed_sums)
    value_grad = jnp.einsum("td,te->de", normed_rows, dv_rows, preferred_element_type=f32)
    query_grad = jnp.einsum(
        "td,te->de", own_rows, after(dq.reshape(-1, D), chip), preferred_element_type=f32
    )
    attn_sum = RowSum(
        jnp.stack([query_grad.astype(bf16), key_grad, value_grad.astype(bf16), output_grad]),
        sum_order("y"),
    )
    attn_sum.start()
    bias_rows = bias_sums(rank_ref, after_sends(near_parts, attn_sum), far_parts, parts)
    attn_sum.finish(bias_rows)
    attn_sum.start()
    from_x = after_sends(after(from_x, bias_rows), attn_sum)
    normed_grad = chip[:, :own] + direct + from_x.astype(f32)
    shared = SumEverywhere(
        jnp.concatenate(
            [
                bias_rows.reshape(HEADS, 128),
                jnp.broadcast_to(jnp.sum(feed_stats[1]), (16 - HEADS, 128)),
            ],
            axis=0,
        )
    )
    shared.start()

    embed_part, small_part = 0.0, 0.0
    for s in range(seqs):
        a, b = pool_back(
            s, first_byte.reshape(1), phase_ids[:, :, None], phase_ids[:, None, :], table,
            normed_grad, residual, after_grad.reshape(seqs, own, D), total_bytes,
        )
        embed_part, small_part = embed_part + a, small_part + b
        attn_sum.finish(b)
        shared.finish(b)
        attn_sum.start()
        shared.start()
        if s < seqs - 1:
            normed_grad = after(after_sends(normed_grad, attn_sum), shared.value)
    front = jnp.concatenate(
        [
            embed_part[:VOCAB],
            small_part[:6],
            feed_stats[:1],
            jnp.zeros((TABLE - VOCAB - 7, D), f32),
        ],
        axis=0,
    )
    front_sum = RowSum(front.T[None], sum_order("x"))
    front_sum = front_sum.result().reshape(shard, TABLE).T
    sums = shared.result()
    bias_grad = sums[:HEADS, :BUCKETS].T
    attn_sum = attn_sum.result()
    gate_sum, up_sum, down_sum = [each.result()[0] for each in (gate_sum, up_sum, down_sum)]

    return (
        block_out.reshape(seqs, own, D),
        sums[HEADS, 0] / live_count,
        front_sum[:VOCAB],
        front_sum[VOCAB : VOCAB + 4],
        front_sum[VOCAB + 4],
        front_sum[VOCAB + 5],
        bias_grad,
        attn_sum[0],
        attn_sum[1],
        attn_sum[2],
        attn_sum[3],
        front_sum[VOCAB + 6],
        gate_sum,
        up_sum,
        down_sum,
    )


def solution(mesh):
    tokens = P("dp", "seq", None)
    features = P(("dp", "seq"))
    columns = P(None, ("dp", "seq"))
    rows = P(("dp", "seq"), None)
    in_specs = (
        P("dp", "seq"), P("dp"), tokens, columns, columns, features, features, P(),
        rows, rows, rows, rows, features, rows, rows, rows,
    )
    out_specs = (
        tokens, P(), columns, columns, features, features, P(), rows, rows, rows, rows,
        features, rows, rows, rows,
    )
    return jax.shard_map(
        per_device, mesh=mesh, in_specs=in_specs, out_specs=out_specs, check_vma=False
    )
```

profile of v0, /device:TPU:0, one launch (start us, length us, event | category | flops | bytes accessed | tf_op | source)
XLA Modules:
  0.0 456.9 jit_solution(3898053036871801134)
XLA Ops:
  15.9 4.1 collective-permute-start
  20.9 2.9 collective-permute-start.5
  35.0 3.4 collective-permute-done.12
  47.3 12.1 %pool.2 = (f32[3,256,768]{2,1,0:T(8,128)}, bf16[3,256,768]{2,1,0:T(8,128)(2,1)}) custom-call(s32[1]{0:T(128)} %bitcast.24.first_ref, s32[3,576,1]{2,1,0:T(8,128)} %broadcast_in_dim_reshape.18.ids, bf16[768,384]{1,0:T(8,128)(2,1)} %bitcast.349), custom_call_target="tpu_custom_call" | custom-call | flops 8999999488 | bytes 4000000 | tf_op jit(solution)/shard_map/pool/pallas_call | solution.py:365
  65.0 12.0 %pool.3 = (f32[3,256,768]{2,1,0:T(8,128)}, bf16[3,256,768]{2,1,0:T(8,128)(2,1)}) custom-call(s32[1]{0:T(128)} %bitcast.36.first_ref, s32[3,576,1]{2,1,0:T(8,128)} %broadcast_in_dim_reshape.17.ids, bf16[768,384]{1,0:T(8,128)(2,1)} %bitcast.350), custom_call_target="tpu_custom_call" | custom-call | flops 8999999488 | bytes 4000000 | tf_op jit(solution)/shard_map/pool/pallas_call | solution.py:365
  79.6 8.4 %prepare.1 = (bf16[12,256,512]{2,1,0:T(8,128)(2,1)}, bf16[12,512,256]{2,1,0:T(8,128)(2,1)}, bf16[3,1024,128]{2,1,0:T(8,128)(2,1)}) custom-call(s32[1]{0:T(128)} %bitcast.23.rank_ref, s32[3]{0:T(128)} %lengths_ref.3, f32[32,12]{1,0:T(8,128)} %copy.189.bias_ref, bf16[32,128]{1,0:T(8,128)(2,1)} %pad.10.lanes_bias), custom_call_target="tpu_custom_call" | custom-call | flops 6000000000 | bytes 7000000 | tf_op jit(solution)/shard_map/prepare/pallas_call | solution.py:622
  97.3 2.1 convolution_convert_fusion.8
  99.9 10.0 %convolution_convert_fusion = bf16[3072,1536]{1,0:T(8,128)(2,1)} fusion(bf16[3072,768]{1,0:T(8,128)(2,1)S(1)} %bitcast.315, bf16[768,1152]{1,0:T(8,128)(2,1)S(1)} %bitcast.306, bf16[768,1152]{1,0:T(8,128)(2,1)S(1)} %bitcast.346), kind=kOutput, calls=%fused_computation.1 | convolution fusion | flops 7257194496 | bytes 17694720 | tf_op jit(solution)/shard_map/dot_general | solution.py:1036
  110.0 27.3 %attend.1 = (bf16[3,256,768]{2,1,0:T(8,128)(2,1)}, f32[3,256,128]{2,1,0:T(8,128)}) custom-call(s32[1]{0:T(128)} %bitcast.23.rank_ref, bf16[3,256,768]{2,1,0:T(8,128)(2,1)} %bitcast.478, bf16[3,1024,1536]{2,1,0:T(8,128)(2,1)} %bitcast.458, bf16[3,1024,1536]{2,1,0:T(8,128)(2,1)} %bitcast.459, bf16[3,1024,128]{2,1,0:T(8,128)(2,1)} %get-tuple-element.105.side, ...), custom_call_target="tpu_custom_call" | custom-call | flops 24999999488 | bytes 8000000 | tf_op jit(solution)/shard_map/attend/pallas_call | solution.py:711
  139.1 2.0 copy.194
  141.1 29.5 %feed.1 = (f32[768,768]{1,0:T(8,128)}, bf16[768,768]{1,0:T(8,128)(2,1)}, bf16[768,2048]{1,0:T(8,128)(2,1)}, bf16[768,768]{1,0:T(8,128)(2,1)}, bf16[768,2048]{1,0...) custom-call(s32[1]{0:T(128)} %bitcast.place_ref, ...), custom_call_target="tpu_custom_call" | custom-call | flops 16999999488 | bytes 30000000 | tf_op jit(solution)/shard_map/feed/pallas_call | solution.py:1000
  170.6 3.6 convolution_convert_fusion.7
  174.2 2.9 convolution_convert_fusion.3
  179.9 2.9 convolution_convert_fusion.2
  182.8 3.1 convolution_convert_fusion.1
  191.6 16.6 %attend_back.3 = (bf16[3,256,768]{2,1,0:T(8,128)(2,1)}, bf16[3,1024,768]{2,1,0:T(8,128)(2,1)}, bf16[3,1024,768]{2,1,0:T(8,128)(2,1)}, bf16[3,12,512,256]{3,2,1,0:T(8,128)(2,1)}, f32[3,12,16,256]{3,2,1,0:T(8,128)}) custom-call(s32[1]{0:T(128)} %bitcast.23.rank_ref, bf16[3,256,768]{2,1,0:T(8,128)(2,1)} %bitcast.479, bf16[3,1024,1536]{2,1,0:T(8,128)(2,1)} %bitcast.460, ...), custom_call_target="tpu_custom_call" | custom-call | flops 15000000512 | bytes 12000000 | tf_op jit(solution)/shard_map/attend_back/pallas_call | solution.py:810
  208.2 2.3 constant_dynamic-slice_fusion.31
  210.5 2.3 add_convert_fusion.1
  212.7 2.2 add_convert_fusion.3
  215.8 2.3 add_convert_fusion.2
  220.6 16.4 %attend_back.4 = (bf16[3,256,768]{2,1,0:T(8,128)(2,1)}, bf16[3,1024,768]{2,1,0:T(8,128)(2,1)}, bf16[3,1024,768]{2,1,0:T(8,128)(2,1)}, bf16[3,12,512,256]{3,2,1,0:T(8,128)(2,1)}, f32[3,12,16,256]{3,2,1,0:T(8,128)}) custom-call(s32[1]{0:T(128)} %bitcast.23.rank_ref, ...), custom_call_target="tpu_custom_call", output_to_operand_aliasing={{0}: (9, {}), {1}: (10, {}), {2}: (11, {}), {3}: (12, {}), ... | custom-call | flops 15000000512 | bytes 12000000 | tf_op jit(solution)/shard_map/attend_back/pallas_call | solution.py:810
  240.4 2.1 fusion.11
  242.5 2.4 collective-permute-start.22
  249.6 16.3 %attend_back.5 = (bf16[3,256,768]{2,1,0:T(8,128)(2,1)}, bf16[3,1024,768]{2,1,0:T(8,128)(2,1)}, bf16[3,1024,768]{2,1,0:T(8,128)(2,1)}, bf16[3,12,512,256]{3,2,1,0:T(8,128)(2,1)}, f32[3,12,16,256]{3,2,1,0:T(8,128)}) custom-call(s32[1]{0:T(128)} %bitcast.23.rank_ref, ...), custom_call_target="tpu_custom_call", output_to_operand_aliasing={{0}: (9, {}), {1}: (10, {}), {2}: (11, {}), {3}: (12, {}), ... | custom-call | flops 15000000512 | bytes 12000000 | tf_op jit(solution)/shard_map/attend_back/pallas_call | solution.py:810
  272.0 6.8 %fusion.6 = f32[3072,768]{1,0:T(8,128)S(1)} fusion(bf16[3072,768]{1,0:T(8,128)(2,1)} %bitcast.466, bf16[768,1152]{1,0:T(8,128)(2,1)S(1)} %bitcast.347, bf16[768,1152]{1,0:T(8,128)(2,1)S(1)} %bitcast.307), kind=kOutput, calls=%fused_computation.32 | convolution fusion | flops 3626237952 | bytes 17694720 | tf_op jit(solution)/shard_map/te,de->td/dot_general | solution.py:1210
  278.8 3.9 convolution_add_fusion
  282.7 3.5 copy-done.2
  287.0 2.0 collective-permute-start.28
  288.9 8.0 %convolution_convert_fusion.6 = bf16[768,768]{1,0:T(8,128)(2,1)S(1)} fusion(bf16[3072,768]{1,0:T(8,128)(2,1)} %bitcast.316, bf16[3072,768]{1,0:T(8,128)(2,1)} %bitcast.467), kind=kOutput, calls=%fused_computation.25 | convolution fusion | flops 3624468480 | bytes 10616832 | tf_op jit(solution)/shard_map/td,te->de/dot_general | solution.py:1218
  299.7 2.0 fusion.17
  303.7 4.4 slice_add_fusion
  308.1 4.2 fusion.4
  317.4 2.0 fusion.33
  319.4 2.9 collective-permute-start.45
  322.4 5.0 %collective-permute-done.46 = bf16[1,24,2048]{2,1,0:T(8,128)(2,1)S(1)} collective-permute-done((bf16[1,24,2048]{2,1,0:T(8,128)(2,1)S(1)}, bf16[1,24,2048]{2,1,0:T(8,128)(2,1)S(1)}, u32[]{:S(2)}, u32[]{:S(2)}) %collective-permute-start.46) | collective-permute-done | bytes 98336 | tf_op jit(solution)/shard_map/ppermute | solution.py:54
  331.3 2.8 slice.223
  336.1 12.8 %bias_sums.1 = f32[12,1,128]{2,1,0:T(1,128)} custom-call(s32[1]{0:T(128)} %bitcast.23.rank_ref, bf16[3,12,512,256]{3,2,1,0:T(8,128)(2,1)} %get-tuple-element.155.near, f32[3,12,16,256]{3,2,1,0:T(8,128)} %get-tuple-element.141.far), custom_call_target="tpu_custom_call" | custom-call | flops 6000000000 | bytes 9000000 | tf_op jit(solution)/shard_map/bias_sums/pallas_call | solution.py:912
  351.8 10.6 %collective-permute-done.30 = bf16[3,256,768]{2,1,0:T(8,128)(2,1)} collective-permute-done((bf16[3,256,768]{2,1,0:T(8,128)(2,1)}, bf16[3,256,768]{2,1,0:T(8,128)(2,1)}, u32[]{:S(2)}, u32[]{:S(2)}) %collective-permute-start.30) | collective-permute-done | bytes 1179680 | tf_op jit(solution)/shard_map/ppermute | solution.py:54
  362.4 2.8 add_convert_fusion
  365.3 4.6 fusion.2.grad_normed
  369.8 10.1 %pool_back.3 = (f32[384,768]{1,0:T(8,128)}, f32[8,768]{1,0:T(8,128)}) custom-call(s32[1]{0:T(128)} %bitcast.24.first_ref, s32[3,576,1]{2,1,0:T(8,128)} %broadcast_in_dim_reshape.18.ids, s32[3,1,576]{2,1,0:T(1,128)} %broadcast_in_dim_reshape.16.ids_row, bf16[768,384]{1,0:T(8,128)(2,1)} %bitcast.353, f32[3,256,768]{2,1,0:T(8,128)} %fusion.2.grad_normed, ...), custom_call_target="tpu_custom_call" | custom-call | flops 8000000000 | bytes 8000000 | tf_op jit(solution)/shard_map/pool_back/pallas_call | solution.py:523
  385.3 7.2 %collective-permute-done.33 = bf16[4,192,768]{2,1,0:T(8,128)(2,1)S(1)} collective-permute-done((bf16[4,192,768]{2,1,0:T(8,128)(2,1)}, bf16[4,192,768]{2,1,0:T(8,128)(2,1)S(1)}, u32[]{:S(2)}, u32[]{:S(2)}) %collective-permute-start.33) | collective-permute-done | bytes 1179680 | tf_op jit(solution)/shard_map/ppermute | solution.py:54
  393.1 10.3 %pool_back.4 = (f32[384,768]{1,0:T(8,128)}, f32[8,768]{1,0:T(8,128)}) custom-call(s32[1]{0:T(128)} %bitcast.24.first_ref, s32[3,576,1]{2,1,0:T(8,128)} %broadcast_in_dim_reshape.18.ids, s32[3,1,576]{2,1,0:T(1,128)} %broadcast_in_dim_reshape.16.ids_row, bf16[768,384]{1,0:T(8,128)(2,1)} %bitcast.354, f32[3,256,768]{2,1,0:T(8,128)} %fusion.2.grad_normed, ...), custom_call_target="tpu_custom_call" | custom-call | flops 8000000000 | bytes 8000000 | tf_op jit(solution)/shard_map/pool_back/pallas_call | solution.py:523
  407.3 10.2 %pool_back.5 = (f32[384,768]{1,0:T(8,128)}, f32[8,768]{1,0:T(8,128)}) custom-call(s32[1]{0:T(128)} %bitcast.24.first_ref, s32[3,576,1]{2,1,0:T(8,128)} %broadcast_in_dim_reshape.18.ids, s32[3,1,576]{2,1,0:T(1,128)} %broadcast_in_dim_reshape.16.ids_row, bf16[768,384]{1,0:T(8,128)(2,1)} %bitcast.355, f32[3,256,768]{2,1,0:T(8,128)} %fusion.2.grad_normed, ...), custom_call_target="tpu_custom_call" | custom-call | flops 8000000000 | bytes 8000000 | tf_op jit(solution)/shard_map/pool_back/pallas_call | solution.py:523
  422.4 4.5 collective-permute-done.37
  430.4 3.6 collective-permute-done.39
  434.6 3.9 collective-permute-done.40
  443.6 3.6 collective-permute-done.42
  (389 shorter events, 116.7 us)
Async XLA Ops:
  7.2 130.0 %all-gather.2.cloned.1.call-start = ((), (), s32[]{:S(2)}) async-start(), calls=%async_computation | async-start | bytes 10948608 | tf_op jit(solution)/shard_map/all_gather | solution.py:1140
  15.9 8.7 %collective-permute-start = (bf16[24,384]{1,0:T(8,128)(2,1)S(1)}, bf16[24,384]{1,0:T(8,128)(2,1)S(1)}, u32[]{:S(2)}, u32[]{:S(2)}) collective-permute-start(bf16[24,384]{1,0:T(8,128)(2,1)S(1)} %bitcast.450), channel_id=1, source_target_pairs={{0,16},{4,20},{8,24},{12,28},{16,0},{20,4},{24,8},{28,12},{1,17},{... | collective-permute-start | bytes 55304 | tf_op jit(solution)/shard_map/ppermute | solution.py:54
  20.8 9.8 %collective-permute-start.11 = (bf16[24,1152]{1,0:T(8,128)(2,1)S(1)}, bf16[24,1152]{1,0:T(8,128)(2,1)S(1)}, u32[]{:S(2)}, u32[]{:S(2)}) collective-permute-start(bf16[24,1152]{1,0:T(8,128)(2,1)S(1)} %get-tuple-element.310), channel_id=1, source_target_pairs={{0,16},{4,20},{8,24},{12,28},{16,0},{20,4},{24,8},{28,12},{1,17},{... | collective-permute-start | bytes 165896 | tf_op jit(solution)/shard_map/ppermute | solution.py:54
  20.9 11.9 %collective-permute-start.5 = (bf16[24,1152]{1,0:T(8,128)(2,1)S(1)}, bf16[24,1152]{1,0:T(8,128)(2,1)S(1)}, u32[]{:S(2)}, u32[]{:S(2)}) collective-permute-start(bf16[24,1152]{1,0:T(8,128)(2,1)S(1)} %get-tuple-element.311), channel_id=1, source_target_pairs={{0,16},{4,20},{8,24},{12,28},{16,0},{20,4},{24,8},{28,12},{1,17},{... | collective-permute-start | bytes 165896 | tf_op jit(solution)/shard_map/ppermute | solution.py:54
  24.6 4.3 collective-permute-start.1
  29.0 4.4 collective-permute-start.2
  30.7 7.8 %collective-permute-start.12 = (bf16[2,24,1152]{2,1,0:T(8,128)(2,1)S(1)}, bf16[2,24,1152]{2,1,0:T(8,128)(2,1)S(1)}, u32[]{:S(2)}, u32[]{:S(2)}) collective-permute-start(bf16[2,24,1152]{2,1,0:T(8,128)(2,1)S(1)} %pad_maximum_fusion.19), channel_id=1, source_target_pairs={{0,8},{4,12},{8,0},{12,4},{16,24},{20,28},{24,16},{28,20},{1,9},{5... | collective-permute-start | bytes 331784 | tf_op jit(solution)/shard_map/ppermute | solution.py:54
  32.8 7.5 %collective-permute-start.6 = (bf16[2,24,1152]{2,1,0:T(8,128)(2,1)S(1)}, bf16[2,24,1152]{2,1,0:T(8,128)(2,1)S(1)}, u32[]{:S(2)}, u32[]{:S(2)}) collective-permute-start(bf16[2,24,1152]{2,1,0:T(8,128)(2,1)S(1)} %pad_maximum_fusion.18), channel_id=1, source_target_pairs={{0,8},{4,12},{8,0},{12,4},{16,24},{20,28},{24,16},{28,20},{1,9},{5... | collective-permute-start | bytes 331784 | tf_op jit(solution)/shard_map/ppermute | solution.py:54
  33.5 6.9 %collective-permute-start.3 = (bf16[200,384]{1,0:T(8,128)(2,1)S(1)}, bf16[200,384]{1,0:T(8,128)(2,1)S(1)}, u32[]{:S(2)}, u32[]{:S(2)}) collective-permute-start(bf16[200,384]{1,0:T(8,128)(2,1)S(1)} %pad_maximum_fusion.16), channel_id=1, source_target_pairs={{0,2},{1,3},{2,0},{3,1},{4,6},{5,7},{6,4},{7,5},{8,10},{9,11},{10,... | collective-permute-start | bytes 460808 | tf_op jit(solution)/shard_map/ppermute | solution.py:54
  40.5 20.6 %collective-permute-start.7 = (bf16[2,2,24,1152]{3,2,0,1:T(8,128)(2,1)S(1)}, bf16[2,2,24,1152]{3,2,0,1:T(8,128)(2,1)S(1)}, u32[]{:S(2)}, u32[]{:S(2)}) collective-permute-start(bf16[2,2,24,1152]{3,2,0,1:T(8,128)(2,1)S(1)} %pad_maximum_fusion.14), channel_id=1, source_target_pairs={{0,4},{4,0},{8,12},{12,8},{16,20},{20,16},{24,28},{28,24},{1,5},{5... | collective-permute-start | bytes 663560 | tf_op jit(solution)/shard_map/ppermute | solution.py:54
  42.1 19.0 %collective-permute-start.13 = (bf16[2,2,24,1152]{3,2,0,1:T(8,128)(2,1)S(1)}, bf16[2,2,24,1152]{3,2,0,1:T(8,128)(2,1)S(1)}, u32[]{:S(2)}, u32[]{:S(2)}) collective-permute-start(bf16[2,2,24,1152]{3,2,0,1:T(8,128)(2,1)S(1)} %pad_maximum_fusion.15), channel_id=1, source_target_pairs={{0,2},{1,3},{2,0},{3,1},{4,6},{5,7},{6,4},{7,5},{8,10},{9,11},{10,... | collective-permute-start | bytes 663560 | tf_op jit(solution)/shard_map/ppermute | solution.py:54
  62.1 25.9 %collective-permute-start.14 = (bf16[2,2,2,24,1152]{4,3,0,1,2:T(8,128)(2,1)}, bf16[2,2,2,24,1152]{4,3,0,1,2:T(8,128)(2,1)}, u32[]{:S(2)}, u32[]{:S(2)}) collective-permute-start(bf16[2,2,2,24,1152]{4,3,0,1,2:T(8,128)(2,1)} %pad_maximum_fusion.11), channel_id=1, source_target_pairs={{0,4},{4,0},{8,12},{12,8},{16,20},{20,16},{24,28},{28,24},{1,5},{5... | collective-permute-start | bytes 1327112 | tf_op jit(solution)/shard_map/ppermute | solution.py:54
  64.1 27.1 %collective-permute-start.8 = (bf16[2,2,2,24,1152]{4,3,0,1,2:T(8,128)(2,1)}, bf16[2,2,2,24,1152]{4,3,0,1,2:T(8,128)(2,1)}, u32[]{:S(2)}, u32[]{:S(2)}) collective-permute-start(bf16[2,2,2,24,1152]{4,3,0,1,2:T(8,128)(2,1)} %pad_maximum_fusion.10), channel_id=1, source_target_pairs={{0,2},{1,3},{2,0},{3,1},{4,6},{5,7},{6,4},{7,5},{8,10},{9,11},{10,... | collective-permute-start | bytes 1327112 | tf_op jit(solution)/shard_map/ppermute | solution.py:54
  89.4 5.6 %collective-permute-start.15 = (bf16[2,2,2,2,24,1152]{5,4,0,1,3,2:T(8,128)(2,1)S(1)}, bf16[2,2,2,2,24,1152]{5,4,0,1,3,2:T(8,128)(2,1)S(1)}, u32[]{:S(2)}, u32[]{:S(2)}) collective-permute-start(bf16[2,2,2,2,24,1152]{5,4,0,1,3,2:T(8,128)(2,1)S(1)} %pad_maximum_fusion.8), channel_id=1, source_target_pairs={{0,1},{1,0},{2,3},{3,2},{4,5},{5,4},{6,7},{7,6},{8,9},{9,8},{10,11... | collective-permute-start | bytes 2654216 | tf_op jit(solution)/shard_map/ppermute | solution.py:54
  90.7 8.7 %collective-permute-start.10 = (bf16[3,512,768]{2,1,0:T(8,128)(2,1)S(1)}, bf16[3,512,768]{2,1,0:T(8,128)(2,1)S(1)}, u32[]{:S(2)}, u32[]{:S(2)}) collective-permute-start(bf16[3,512,768]{2,1,0:T(8,128)(2,1)S(1)} %pad_maximum_fusion.2), channel_id=1, source_target_pairs={{0,1},{1,0},{2,3},{3,2},{4,5},{5,4},{6,7},{7,6},{8,9},{9,8},{10,11... | collective-permute-start | bytes 7077896 | tf_op jit(solution)/shard_map/ppermute | solution.py:54
  92.5 4.3 collective-permute-start.9
  178.5 34.2 %collective-permute-start.16 = (bf16[1,1024,768]{2,1,0:T(8,128)(2,1)}, bf16[1,1024,768]{2,1,0:T(8,128)(2,1)}, u32[]{:S(2)}, u32[]{:S(2)}) collective-permute-start(bf16[1,1024,768]{2,1,0:T(8,128)(2,1)} %bitcast.68), channel_id=1, source_target_pairs={{0,1},{1,0},{2,3},{3,2},{4,5},{5,4},{6,7},{7,6},{8,9},{9,8},{10,11... | collective-permute-start | bytes 4718600 | tf_op jit(solution)/shard_map/ppermute | solution.py:54
  190.2 17.9 %collective-permute-start.18 = (bf16[1,384,2048]{2,1,0:T(8,128)(2,1)}, bf16[1,384,2048]{2,1,0:T(8,128)(2,1)}, u32[]{:S(2)}, u32[]{:S(2)}) collective-permute-start(bf16[1,384,2048]{2,1,0:T(8,128)(2,1)} %bitcast.72), channel_id=1, source_target_pairs={{0,1},{1,0},{2,3},{3,2},{4,5},{5,4},{6,7},{7,6},{8,9},{9,8},{10,11... | collective-permute-start | bytes 4718600 | tf_op jit(solution)/shard_map/ppermute | solution.py:54
  190.5 17.7 %collective-permute-start.17 = (bf16[1,384,2048]{2,1,0:T(8,128)(2,1)}, bf16[1,384,2048]{2,1,0:T(8,128)(2,1)}, u32[]{:S(2)}, u32[]{:S(2)}) collective-permute-start(bf16[1,384,2048]{2,1,0:T(8,128)(2,1)} %bitcast.70), channel_id=1, source_target_pairs={{0,1},{1,0},{2,3},{3,2},{4,5},{5,4},{6,7},{7,6},{8,9},{9,8},{10,11... | collective-permute-start | bytes 4718600 | tf_op jit(solution)/shard_map/ppermute | solution.py:54
  214.9 25.4 %collective-permute-start.19 = (bf16[1,512,768]{2,1,0:T(8,128)(2,1)}, bf16[1,512,768]{2,1,0:T(8,128)(2,1)}, u32[]{:S(2)}, u32[]{:S(2)}) collective-permute-start(bf16[1,512,768]{2,1,0:T(8,128)(2,1)} %bitcast.76), channel_id=1, source_target_pairs={{0,8},{4,12},{8,0},{12,4},{16,24},{20,28},{24,16},{28,20},{1,9},{5... | collective-permute-start | bytes 2359304 | tf_op jit(solution)/shard_map/ppermute | solution.py:54
  218.1 26.8 %collective-permute-start.20 = (bf16[1,192,2048]{2,1,0:T(8,128)(2,1)}, bf16[1,192,2048]{2,1,0:T(8,128)(2,1)S(1)}, u32[]{:S(2)}, u32[]{:S(2)}) collective-permute-start(bf16[1,192,2048]{2,1,0:T(8,128)(2,1)} %bitcast.79), channel_id=1, source_target_pairs={{0,2},{1,3},{2,0},{3,1},{4,6},{5,7},{6,4},{7,5},{8,10},{9,11},{10,... | collective-permute-start | bytes 2359304 | tf_op jit(solution)/shard_map/ppermute | solution.py:54
  219.5 26.5 %collective-permute-start.21 = (bf16[1,192,2048]{2,1,0:T(8,128)(2,1)}, bf16[1,192,2048]{2,1,0:T(8,128)(2,1)}, u32[]{:S(2)}, u32[]{:S(2)}) collective-permute-start(bf16[1,192,2048]{2,1,0:T(8,128)(2,1)} %bitcast.82), channel_id=1, source_target_pairs={{0,4},{4,0},{8,12},{12,8},{16,20},{20,16},{24,28},{28,24},{1,5},{5... | collective-permute-start | bytes 2359304 | tf_op jit(solution)/shard_map/ppermute | solution.py:54
  242.5 27.1 %collective-permute-start.22 = (bf16[1,256,768]{2,1,0:T(8,128)(2,1)}, bf16[1,256,768]{2,1,0:T(8,128)(2,1)S(1)}, u32[]{:S(2)}, u32[]{:S(2)}) collective-permute-start(bf16[1,256,768]{2,1,0:T(8,128)(2,1)} %fusion.11), channel_id=1, source_target_pairs={{0,16},{4,20},{8,24},{12,28},{16,0},{20,4},{24,8},{28,12},{1,17},{... | collective-permute-start | bytes 1179656 | tf_op jit(solution)/shard_map/ppermute | solution.py:54
  245.0 24.5 %collective-permute-start.23 = (bf16[1,96,2048]{2,1,0:T(8,128)(2,1)S(1)}, bf16[1,96,2048]{2,1,0:T(8,128)(2,1)S(1)}, u32[]{:S(2)}, u32[]{:S(2)}) collective-permute-start(bf16[1,96,2048]{2,1,0:T(8,128)(2,1)S(1)} %bitcast.418), channel_id=1, source_target_pairs={{0,4},{4,0},{8,12},{12,8},{16,20},{20,16},{24,28},{28,24},{1,5},{5... | collective-permute-start | bytes 1179656 | tf_op jit(solution)/shard_map/ppermute | solution.py:54
  247.8 21.8 %collective-permute-start.24 = (bf16[1,96,2048]{2,1,0:T(8,128)(2,1)}, bf16[1,96,2048]{2,1,0:T(8,128)(2,1)S(1)}, u32[]{:S(2)}, u32[]{:S(2)}) collective-permute-start(bf16[1,96,2048]{2,1,0:T(8,128)(2,1)} %bitcast.92), channel_id=1, source_target_pairs={{0,2},{1,3},{2,0},{3,1},{4,6},{5,7},{6,4},{7,5},{8,10},{9,11},{10,... | collective-permute-start | bytes 1179656 | tf_op jit(solution)/shard_map/ppermute | solution.py:54
  286.5 17.2 %collective-permute-start.25 = (bf16[3,512,768]{2,1,0:T(8,128)(2,1)S(1)}, bf16[3,512,768]{2,1,0:T(8,128)(2,1)}, u32[]{:S(2)}, u32[]{:S(2)}) collective-permute-start(bf16[3,512,768]{2,1,0:T(8,128)(2,1)S(1)} %slice.222), channel_id=1, source_target_pairs={{0,1},{1,0},{2,3},{3,2},{4,5},{5,4},{6,7},{7,6},{8,9},{9,8},{10,11... | collective-permute-start | bytes 7077896 | tf_op jit(solution)/shard_map/ppermute | solution.py:54
  286.6 11.7 %collective-permute-start.27 = (bf16[1,48,2048]{2,1,0:T(8,128)(2,1)}, bf16[1,48,2048]{2,1,0:T(8,128)(2,1)S(1)}, u32[]{:S(2)}, u32[]{:S(2)}) collective-permute-start(bf16[1,48,2048]{2,1,0:T(8,128)(2,1)} %bitcast.431), channel_id=1, source_target_pairs={{0,8},{4,12},{8,0},{12,4},{16,24},{20,28},{24,16},{28,20},{1,9},{5... | collective-permute-start | bytes 589832 | tf_op jit(solution)/shard_map/ppermute | solution.py:54
  286.7 11.6 %collective-permute-start.26 = (bf16[1,128,768]{2,1,0:T(8,128)(2,1)}, bf16[1,128,768]{2,1,0:T(8,128)(2,1)S(1)}, u32[]{:S(2)}, u32[]{:S(2)}) collective-permute-start(bf16[1,128,768]{2,1,0:T(8,128)(2,1)} %bitcast.430), channel_id=1, source_target_pairs={{0,2},{1,3},{2,0},{3,1},{4,6},{5,7},{6,4},{7,5},{8,10},{9,11},{10,... | collective-permute-start | bytes 589832 | tf_op jit(solution)/shard_map/ppermute | solution.py:54
  287.0 11.3 %collective-permute-start.28 = (bf16[1,48,2048]{2,1,0:T(8,128)(2,1)}, bf16[1,48,2048]{2,1,0:T(8,128)(2,1)S(1)}, u32[]{:S(2)}, u32[]{:S(2)}) collective-permute-start(bf16[1,48,2048]{2,1,0:T(8,128)(2,1)} %bitcast.432), channel_id=1, source_target_pairs={{0,8},{4,12},{8,0},{12,4},{16,24},{20,28},{24,16},{28,20},{1,9},{5... | collective-permute-start | bytes 589832 | tf_op jit(solution)/shard_map/ppermute | solution.py:54
  316.0 46.4 %collective-permute-start.31 = (bf16[4,384,768]{2,1,0:T(8,128)(2,1)}, bf16[4,384,768]{2,1,0:T(8,128)(2,1)}, u32[]{:S(2)}, u32[]{:S(2)}) collective-permute-start(bf16[4,384,768]{2,1,0:T(8,128)(2,1)} %bitcast.123), channel_id=1, source_target_pairs={{0,1},{1,0},{2,3},{3,2},{4,5},{5,4},{6,7},{7,6},{8,9},{9,8},{10,11... | collective-permute-start | bytes 7077896 | tf_op jit(solution)/shard_map/ppermute | solution.py:54
  317.4 10.1 %collective-permute-start.46 = (bf16[1,24,2048]{2,1,0:T(8,128)(2,1)S(1)}, bf16[1,24,2048]{2,1,0:T(8,128)(2,1)S(1)}, u32[]{:S(2)}, u32[]{:S(2)}) collective-permute-start(bf16[1,24,2048]{2,1,0:T(8,128)(2,1)S(1)} %copy-done.55), channel_id=1, source_target_pairs={{0,16},{4,20},{8,24},{12,28},{16,0},{20,4},{24,8},{28,12},{1,17},{... | collective-permute-start | bytes 294920 | tf_op jit(solution)/shard_map/ppermute | solution.py:54
  319.4 10.1 %collective-permute-start.45 = (bf16[1,24,2048]{2,1,0:T(8,128)(2,1)S(1)}, bf16[1,24,2048]{2,1,0:T(8,128)(2,1)S(1)}, u32[]{:S(2)}, u32[]{:S(2)}) collective-permute-start(bf16[1,24,2048]{2,1,0:T(8,128)(2,1)S(1)} %copy-done.54), channel_id=1, source_target_pairs={{0,16},{4,20},{8,24},{12,28},{16,0},{20,4},{24,8},{28,12},{1,17},{... | collective-permute-start | bytes 294920 | tf_op jit(solution)/shard_map/ppermute | solution.py:54
  322.3 12.0 %collective-permute-start.47 = (bf16[1,64,768]{2,1,0:T(8,128)(2,1)S(1)}, bf16[1,64,768]{2,1,0:T(8,128)(2,1)S(1)}, u32[]{:S(2)}, u32[]{:S(2)}) collective-permute-start(bf16[1,64,768]{2,1,0:T(8,128)(2,1)S(1)} %fusion.16), channel_id=1, source_target_pairs={{0,4},{4,0},{8,12},{12,8},{16,20},{20,16},{24,28},{28,24},{1,5},{5... | collective-permute-start | bytes 294920 | tf_op jit(solution)/shard_map/ppermute | solution.py:54
  334.1 28.3 %collective-permute-start.30 = (bf16[3,256,768]{2,1,0:T(8,128)(2,1)}, bf16[3,256,768]{2,1,0:T(8,128)(2,1)}, u32[]{:S(2)}, u32[]{:S(2)}) collective-permute-start(bf16[3,256,768]{2,1,0:T(8,128)(2,1)} %slice.223), channel_id=1, source_target_pairs={{0,2},{1,3},{2,0},{3,1},{4,6},{5,7},{6,4},{7,5},{8,10},{9,11},{10,... | collective-permute-start | bytes 3538952 | tf_op jit(solution)/shard_map/ppermute | solution.py:54
  350.8 29.1 %collective-permute-start.29 = (f32[16,128]{1,0:T(8,128)}, f32[16,128]{1,0:T(8,128)S(1)}, u32[]{:S(2)}, u32[]{:S(2)}) collective-permute-start(f32[16,128]{1,0:T(8,128)} %concatenate.50), channel_id=1, source_target_pairs={{0,1},{1,0},{2,3},{3,2},{4,5},{5,4},{6,7},{7,6},{8,9},{9,8},{10,11... | collective-permute-start | bytes 24584 | tf_op jit(solution)/shard_map/ppermute | solution.py:54
  365.2 27.3 %collective-permute-start.33 = (bf16[4,192,768]{2,1,0:T(8,128)(2,1)}, bf16[4,192,768]{2,1,0:T(8,128)(2,1)S(1)}, u32[]{:S(2)}, u32[]{:S(2)}) collective-permute-start(bf16[4,192,768]{2,1,0:T(8,128)(2,1)} %bitcast.127), channel_id=1, source_target_pairs={{0,4},{4,0},{8,12},{12,8},{16,20},{20,16},{24,28},{28,24},{1,5},{5... | collective-permute-start | bytes 3538952 | tf_op jit(solution)/shard_map/ppermute | solution.py:54
  381.9 21.5 %collective-permute-start.32 = (f32[16,128]{1,0:T(8,128)S(1)}, f32[16,128]{1,0:T(8,128)S(1)}, u32[]{:S(2)}, u32[]{:S(2)}) collective-permute-start(f32[16,128]{1,0:T(8,128)S(1)} %pad_add_fusion.1), channel_id=1, source_target_pairs={{0,2},{1,3},{2,0},{3,1},{4,6},{5,7},{6,4},{7,5},{8,10},{9,11},{10,... | collective-permute-start | bytes 24584 | tf_op jit(solution)/shard_map/ppermute | solution.py:54
  392.7 13.6 %collective-permute-start.35 = (bf16[4,96,768]{2,1,0:T(8,128)(2,1)S(1)}, bf16[4,96,768]{2,1,0:T(8,128)(2,1)S(1)}, u32[]{:S(2)}, u32[]{:S(2)}) collective-permute-start(bf16[4,96,768]{2,1,0:T(8,128)(2,1)S(1)} %bitcast.401), channel_id=1, source_target_pairs={{0,2},{1,3},{2,0},{3,1},{4,6},{5,7},{6,4},{7,5},{8,10},{9,11},{10,... | collective-permute-start | bytes 1769480 | tf_op jit(solution)/shard_map/ppermute | solution.py:54
  403.4 14.8 %collective-permute-start.34 = (f32[16,128]{1,0:T(8,128)S(1)}, f32[16,128]{1,0:T(8,128)S(1)}, u32[]{:S(2)}, u32[]{:S(2)}) collective-permute-start(f32[16,128]{1,0:T(8,128)S(1)} %add.1368), channel_id=1, source_target_pairs={{0,4},{4,0},{8,12},{12,8},{16,20},{20,16},{24,28},{28,24},{1,5},{5... | collective-permute-start | bytes 24584 | tf_op jit(solution)/shard_map/ppermute | solution.py:54
  407.2 21.5 %collective-permute-start.43 = (bf16[4,48,768]{2,1,0:T(8,128)(2,1)}, bf16[4,48,768]{2,1,0:T(8,128)(2,1)}, u32[]{:S(2)}, u32[]{:S(2)}) collective-permute-start(bf16[4,48,768]{2,1,0:T(8,128)(2,1)} %bitcast.137), channel_id=1, source_target_pairs={{0,8},{4,12},{8,0},{12,4},{16,24},{20,28},{24,16},{28,20},{1,9},{5... | collective-permute-start | bytes 884744 | tf_op jit(solution)/shard_map/ppermute | solution.py:54
  418.3 4.0 collective-permute-start.36
  422.2 6.5 %collective-permute-start.38 = (bf16[1,384,384]{2,1,0:T(8,128)(2,1)S(1)}, bf16[1,384,384]{2,1,0:T(8,128)(2,1)S(1)}, u32[]{:S(2)}, u32[]{:S(2)}) collective-permute-start(bf16[1,384,384]{2,1,0:T(8,128)(2,1)S(1)} %bitcast.428), channel_id=1, source_target_pairs={{0,1},{1,0},{2,3},{3,2},{4,5},{5,4},{6,7},{7,6},{8,9},{9,8},{10,11... | collective-permute-start | bytes 884744 | tf_op jit(solution)/shard_map/ppermute | solution.py:54
  422.3 4.6 %collective-permute-start.37 = (f32[16,128]{1,0:T(8,128)S(1)}, f32[16,128]{1,0:T(8,128)S(1)}, u32[]{:S(2)}, u32[]{:S(2)}) collective-permute-start(f32[16,128]{1,0:T(8,128)S(1)} %add.1374), channel_id=1, source_target_pairs={{0,16},{4,20},{8,24},{12,28},{16,0},{20,4},{24,8},{28,12},{1,17},{... | collective-permute-start | bytes 24584 | tf_op jit(solution)/shard_map/ppermute | solution.py:54
  428.8 5.2 %collective-permute-start.39 = (bf16[1,192,384]{2,1,0:T(8,128)(2,1)S(1)}, bf16[1,192,384]{2,1,0:T(8,128)(2,1)S(1)}, u32[]{:S(2)}, u32[]{:S(2)}) collective-permute-start(bf16[1,192,384]{2,1,0:T(8,128)(2,1)S(1)} %bitcast.441), channel_id=1, source_target_pairs={{0,2},{1,3},{2,0},{3,1},{4,6},{5,7},{6,4},{7,5},{8,10},{9,11},{10,... | collective-permute-start | bytes 442376 | tf_op jit(solution)/shard_map/ppermute | solution.py:54
  430.3 9.8 %collective-permute-start.44 = (bf16[4,24,768]{2,1,0:T(8,128)(2,1)S(1)}, bf16[4,24,768]{2,1,0:T(8,128)(2,1)S(1)}, u32[]{:S(2)}, u32[]{:S(2)}) collective-permute-start(bf16[4,24,768]{2,1,0:T(8,128)(2,1)S(1)} %fusion.15), channel_id=1, source_target_pairs={{0,16},{4,20},{8,24},{12,28},{16,0},{20,4},{24,8},{28,12},{1,17},{... | collective-permute-start | bytes 442376 | tf_op jit(solution)/shard_map/ppermute | solution.py:54
  434.0 4.4 collective-permute-start.40
  438.5 4.0 collective-permute-start.41
  442.5 4.7 %collective-permute-start.42 = (bf16[1,24,384]{2,1,0:T(8,128)(2,1)S(1)}, bf16[1,24,384]{2,1,0:T(8,128)(2,1)S(1)}, u32[]{:S(2)}, u32[]{:S(2)}) collective-permute-start(bf16[1,24,384]{2,1,0:T(8,128)(2,1)S(1)} %fusion.20), channel_id=1, source_target_pairs={{0,16},{4,20},{8,24},{12,28},{16,0},{20,4},{24,8},{28,12},{1,17},{... | collective-permute-start | bytes 55304 | tf_op jit(solution)/shard_map/ppermute | solution.py:54
  (79 other events, 606.7 us)
Sparse Core Ops, SparseCore 0:
  10.9 98.1 all-gather.1
where the time goes:
time: 462 us; the launch traced here: 457 us
  Pallas kernels  182 us (39%)
  other arithmetic  55.3 us (12%)
  local copies, waits for them, and re-layouts  53.3 us (12%)
  matrix products  53.1 us (11%)
  waiting for transfers between devices  51.9 us (11%)
  starting transfers between devices  41.8 us (9%)
  between operations  19.7 us (4%)
    ppermute x48, waiting for transfers between devices, swap(): return lax.ppermute(value, axis, [(i, i ^ bit) for i in range(peers)])  51.9 us
    pallas_call x3, Pallas kernels, attend_back(): pl.pallas_call(partial(attend_back_kernel, near=near, blocks=blocks, part...  49.3 us
    ppermute x48, starting transfers between devices, swap(): return lax.ppermute(value, axis, [(i, i ^ bit) for i in range(peers)])  41.7 us
    pallas_call x3, Pallas kernels, pool_back(): pl.pallas_call(partial(pool_back_kernel, rows=rows, total_bytes=total_byt...  30.5 us
    pallas_call x1, Pallas kernels, feed(): pl.pallas_call(partial(feed_kernel, chunk=512), grid=(seqs,), in_specs=[s...  29.5 us
    pallas_call x1, Pallas kernels, attend(): pl.pallas_call(partial(attend_kernel, near=near, blocks=blocks), grid=(se...  27.3 us
    pallas_call x2, Pallas kernels, pool(): pl.pallas_call(partial(pool_kernel, rows=rows, total_bytes=total_bytes),...  24.1 us
    convert_element_type x15, other arithmetic, start(): self.sent = send.astype(bf16)  20.4 us
  transfers between devices with their start and end apart: 49, of which 17 were waited for; matrix products, arithmetic and copies ran while one was open for 24% of the time, Pallas kernels for 33%

commit v1 on v0

--- a/solution.py
+++ b/solution.py
@@ -19,6 +19,7 @@
 LEFT = 20
 RIGHT = 21
 HALF = 128
+KEY_PART = 1024
 
 epsilon = 1e-06
 thresholds = (12, 16, 23, 32, 46, 64, 91)
@@ -120,13 +121,17 @@
     return lax.optimization_barrier((value,) + others)[0]
 
 
+def hold(value, other):
+    return value + (other[(0,) * other.ndim] * 0).astype(value.dtype)
+
+
 def sum_order(first):
     seq, dp = axis_bits("seq")[::-1], axis_bits("dp")[::-1]
     if first == "x":
         return seq + dp
     if first == "y":
         return seq[:1] + dp[:1] + seq[1:] + dp[1:]
-    return seq[:1] + dp[1:] + seq[1:] + dp[:1]
+    return seq[:1] + dp[1:] + dp[:1] + seq[1:]
 
 
 class RowSum:
@@ -156,9 +161,10 @@
         self.parts = [half(value, mine) for value in self.parts]
         self.got = swap(self.sent, axis, bit)
 
-    def finish(self, *others):
+    def finish(self, other=None, hard=False):
         if self.got is not None:
-            self.parts.append(after(self.got, *others) if others else self.got)
+            order = hold if hard else after
+            self.parts.append(self.got if other is None else order(self.got, other))
             self.got = None
 
     def result(self):
@@ -197,27 +203,122 @@
         return self.value
 
 
+def pack_kernel(
+    rank_ref, lengths_ref, table, taps, scorer, gain_a, gain_f, query, key, value, gate, up, down,
+    output, columns, first_half, second_half, packed, rows, *, total_tokens,
+):
+    shard = table.shape[1]
+    live = jnp.int32(0)
+    for s in range(lengths_ref.shape[0]):
+        live += jnp.minimum((lengths_ref[s] + 1) // 2, total_tokens)
+    live = jnp.where(rank_ref[0] == 0, live, 0)
+    first = lax.broadcasted_iota(jnp.int32, (1, shard), 1) == 0
+    rows[...] = jnp.zeros_like(rows)
+    rows[0:VOCAB, 0:shard] = table[...].astype(f32)
+    rows[VOCAB : VOCAB + 4, 0:shard] = taps[...].astype(f32)
+    for i, vector in enumerate((scorer, gain_a, gain_f)):
+        rows[VOCAB + 4 + i : VOCAB + 5 + i, 0:shard] = vector[...].astype(f32)
+    for i, part in enumerate((live // 64, live % 64)):
+        at = VOCAB + 7 + i
+        rows[at : at + 1, 0:shard] = jnp.where(first, part, 0).astype(f32)
+    columns[...] = rows[...].T[0:shard, :].astype(bf16)
+
+    pieces = [query[:, i * SIDE : (i + 1) * SIDE] for i in range(PAIRS)]
+    for i in range(PAIRS):
+        pieces += [key[:, i * SIDE : (i + 1) * SIDE], value[:, i * SIDE : (i + 1) * SIDE]]
+    for half in (first_half, second_half):
+        count = half.shape[1] // SIDE
+        for i in range(count):
+            half[:, i * SIDE : (i + 1) * SIDE] = pieces.pop(0)
+
+    ffn_dim = gate.shape[1]
+    packed[:, 0:ffn_dim] = gate[...]
+    packed[:, ffn_dim : 2 * ffn_dim] = up[...]
+    packed[:, 3 * ffn_dim :] = output[...]
+    third = D // 3
+    wide = down[...].astype(f32)
+    for group in range(down.shape[0] // 64):
+        for i in range(8):
+            at = group * 64 + i * 8
+            tiles = [wide[at : at + 8, j * third : (j + 1) * third] for j in range(3)]
+            start = 2 * ffn_dim + i * third
+            packed[group * 24 : (group + 1) * 24, start : start + third] = jnp.concatenate(
+                tiles, axis=0
+            ).astype(bf16)
+
+
+def pack(rank, lengths, table, taps, vectors, attn, feed_weights, total_tokens):
+    smem = pl.BlockSpec(memory_space=pltpu.SMEM)
+    vmem = pl.BlockSpec(memory_space=pltpu.VMEM)
+    shard, ffn_dim = table.shape[1], feed_weights[0].shape[1]
+    shapes = [(shard, TABLE), (shard, 3 * D // 2), (shard, 3 * D // 2), (shard, 3 * ffn_dim + D)]
+    return pl.pallas_call(
+        partial(pack_kernel, total_tokens=total_tokens),
+        in_specs=[smem, smem] + [vmem] * 12,
+        out_specs=[vmem] * 4,
+        out_shape=[jax.ShapeDtypeStruct(shape, bf16) for shape in shapes],
+        scratch_shapes=[pltpu.VMEM((TABLE, -(-shard // 128) * 128), f32)],
+        cost_estimate=pl.CostEstimate(flops=100_000_000, bytes_accessed=1_000_000, transcendentals=0),
+        name="pack",
+    )(rank, lengths, table, taps, *vectors, *attn, *feed_weights)
+
+
+def pack_plain(rank, lengths, table, taps, vectors, attn, feed_weights, total_tokens):
+    shard = table.shape[1]
+    live = jnp.sum(jnp.minimum((lengths + 1) // 2, total_tokens))
+    live = jnp.where(rank[0] == 0, live, 0)
+    counts = jnp.stack([live // 64, live % 64])
+    at_count = (jnp.arange(shard) == 0).astype(jnp.int32)
+    columns = jnp.concatenate(
+        [table, taps, *vectors, (counts[:, None] * at_count[None]).astype(bf16)], axis=0
+    )
+    columns = jnp.pad(columns, ((0, TABLE - columns.shape[0]), (0, 0))).T
+    query, key, value = attn
+    pairs = jnp.stack([key.reshape(shard, PAIRS, SIDE), value.reshape(shard, PAIRS, SIDE)], axis=2)
+    rows = jnp.concatenate([query, pairs.reshape(shard, 2 * D)], axis=1)
+    gate, up, down, output = feed_weights
+    packed = jnp.concatenate([gate, up, down.reshape(shard, gate.shape[1]), output], axis=1)
+    return columns, rows[:, : 3 * D // 2], rows[:, 3 * D // 2 :], packed
+
+
 def up(x):
     return pltpu.roll(x, x.shape[0] - 1, 0)
 
 
 def down(x):
     return pltpu.roll(x, 1, 0)
+
+
+def ahead_lane(x):
+    return pltpu.roll(x, x.shape[1] - 1, 1)
+
+
+def behind_lane(x):
+    return pltpu.roll(x, 1, 1)
 
 
 def triples(c, m0, m1):
     c0, c1, c2, c3 = c
     p01, p23 = c0 + c1, c2 + c3
-    t0, t1, t2, t3 = down(c3) + p01, p01 + c2, c1 + p23, p23 + up(c0)
-    before, after = (down(t3), t0, t1, t2), (t1, t2, t3, up(t0))
+    t0, t1, t2, t3 = behind_lane(c3) + p01, p01 + c2, c1 + p23, p23 + ahead_lane(c0)
+    before, after = (behind_lane(t3), t0, t1, t2), (t1, t2, t3, ahead_lane(t0))
     here = (t0, t1, t2, t3)
     return tuple(
         jnp.where(m0[k], after[k], jnp.where(m1[k], here[k], before[k])) for k in range(4)
     )
 
 
-def position_marks(first, rows, total_bytes):
+def live_rows(first, rows, total_bytes):
     row = lax.broadcasted_iota(jnp.int32, (rows, 128), 0)
+    live = []
+    for k in range(4):
+        pos = first + 4 * (row - 8) + k
+        live.append(((pos >= 0) & (pos < total_bytes)).astype(f32))
+    return live
+
+
+def lane_marks(first, wide, total_bytes):
+    row = lax.broadcasted_iota(jnp.int32, (1, wide), 1)
     live, m0, m1 = [], [], []
     for k in range(4):
         pos = first + 4 * (row - 8) + k
@@ -230,6 +331,26 @@
     return live, m0, m1
 
 
+def to_lanes(accs, count, flat):
+    rows = accs.shape[1]
+    lane = lax.broadcasted_iota(jnp.int32, (rows, 128), 1)
+    value = jnp.zeros((rows, 128), f32)
+    for k in range(count):
+        value = jnp.where(lane == k, jnp.sum(accs[k], axis=-1, keepdims=True), value)
+    flat[0:rows, :] = value
+    turned = flat[...].T
+    return [turned[k : k + 1, :] for k in range(count)]
+
+
+def to_rows(lines, lines_ref, accs):
+    rows = accs.shape[1]
+    for k, line in enumerate(lines):
+        lines_ref[k : k + 1, :] = line
+    turned = lines_ref[...].T
+    for k in range(len(lines)):
+        accs[k] = jnp.broadcast_to(turned[0:rows, k : k + 1], (rows, 128))
+
+
 def lane_chunk(i):
     return pl.ds(pl.multiple_of(i * 128, 128), 128)
 
@@ -245,11 +366,7 @@
     small[...] = nt((lane == row + VOCAB).astype(bf16), table)
 
 
-def all_lanes(x):
-    return jnp.broadcast_to(jnp.sum(x, axis=-1, keepdims=True), x.shape)
-
-
-def block_probs(emb, small, conv, accs, live, m0, m1, rows):
+def block_probs(emb, small, conv, accs, flat, live, m0, m1, rows):
     accs[0:4] = jnp.zeros((4, rows, 128), f32)
 
     def step(i, _):
@@ -271,7 +388,7 @@
         return 0
 
     lax.fori_loop(0, D // 128, step, 0)
-    score = [all_lanes(accs[k]) for k in range(4)]
+    score = to_lanes(accs, 4, flat)
     three = triples(score, m0, m1)
     p01, p23 = score[0] + score[1], score[2] + score[3]
     quad = 0.25 * (p01 + p23)
@@ -329,16 +446,21 @@
     return ((down(c2), down(c3), c0, c1, c2, c3), (c0, c1, c2, c3, up(c0), up(c1)))
 
 
-def pool_kernel(first_ref, ids, table, resid, normed, emb, small, conv, accs, tokens, *, rows, total_bytes):
+def pool_kernel(first_ref, ids, table, resid, normed, emb, small, conv, accs, flat, lines, tokens, *, rows, total_bytes):
     first = first_ref[0]
     embed_bytes(ids[...], table[...], emb)
     small_rows(table[...], small)
-    live, m0, m1 = position_marks(first, rows, total_bytes)
-    probs = block_probs(emb, small, conv, accs, live, m0, m1, rows)
+
+    @pl.when(pl.program_id(0) == 0)
+    def _():
+        flat[...] = jnp.zeros_like(flat)
+        lines[...] = jnp.zeros_like(lines)
+
+    _, m0, m1 = lane_marks(first, flat.shape[0], total_bytes)
+    live = live_rows(first, rows, total_bytes)
+    probs = block_probs(emb, small, conv, accs, flat, live, m0, m1, rows)
     weights = token_weights(probs, m0, m1)
-    for half in range(2):
-        for j in range(6):
-            accs[6 * half + j] = 0.5 * weights[half][j]
+    to_rows([0.5 * weights[half][j] for half in range(2) for j in range(6)], lines, accs)
     own = rows - 16
 
     def step(i, square):
@@ -383,6 +505,8 @@
             pltpu.VMEM((8, D), f32),
             pltpu.VMEM((4, rows, D), f32),
             pltpu.VMEM((12, rows, 128), f32),
+            pltpu.VMEM((2 * 128, 128), f32),
+            pltpu.VMEM((16, 2 * 128), f32),
             pltpu.VMEM((D // 128, tokens, 128), f32),
         ],
         cost_estimate=pl.CostEstimate(flops=count * 3_000_000_000, bytes_accessed=4_000_000, transcendentals=0),
@@ -391,23 +515,40 @@
 
 
 def pool_back_kernel(
-    first_ref, ids, ids_row, table, grad_normed, resid, after, embed_grad, small_grad,
-    emb, small, conv, accs, tokens, pulls, emb_grad, *, rows, total_bytes,
+    first_ref, ids, ids_row, table, pulled_own, from_core, from_x, dq, query_w, resid, after,
+    feed_stats, *rest, rows, total_bytes, given, last, deps,
 ):
+    if given:
+        embed_before, small_before = rest[:2]
+        rest = rest[2:]
+    rest = rest[deps:]
+    if last:
+        turned = rest[0]
+        embed_grad, small_grad = rest[-2:]
+        rest = rest[1:-2]
+    else:
+        embed_grad, small_grad = rest[:2]
+        rest = rest[2:]
+    emb, small, conv, accs, flat, lines, tokens, pulls, emb_grad = rest
     first = first_ref[0]
     own = rows - 16
     chunks = D // 128
 
-    @pl.when(pl.program_id(0) == 0)
-    def _():
-        embed_grad[...] = jnp.zeros_like(embed_grad)
+    if given:
+        small_grad[...] = small_before[...]
+    else:
         small_grad[...] = jnp.zeros_like(small_grad)
+    flat[...] = jnp.zeros_like(flat)
+    lines[...] = jnp.zeros_like(lines)
 
     embed_bytes(ids[...], table[...], emb)
     small_rows(table[...], small)
-    live, m0, m1 = position_marks(first, rows, total_bytes)
-
-    x, gn = resid[...], grad_normed[...]
+    live_lane, m0, m1 = lane_marks(first, flat.shape[0], total_bytes)
+    live = live_rows(first, rows, total_bytes)
+
+    x = resid[...]
+    gn = pulled_own[...].astype(f32) + from_core[...].astype(f32) + from_x[...].astype(f32)
+    gn = gn + nt(dq[...], query_w[...])
     scale = lax.rsqrt(jnp.mean(x * x, axis=-1, keepdims=True) + epsilon)
     gain = small[5:6, :]
     small_grad[5:6, :] += jnp.sum(gn * x * scale, axis=0, keepdims=True)
@@ -417,7 +558,7 @@
     for i in range(chunks):
         tokens[i] = total[:, i * 128 : (i + 1) * 128]
 
-    probs = block_probs(emb, small, conv, accs, live, m0, m1, rows)
+    probs = block_probs(emb, small, conv, accs, flat, live, m0, m1, rows)
     accs[0:12] = jnp.zeros((12, rows, 128), f32)
     pulls[:, 0:8, :] = jnp.zeros((2, 8, D), f32)
     pulls[:, rows - 8 : rows, :] = jnp.zeros((2, 8, D), f32)
@@ -433,9 +574,10 @@
         return 0
 
     lax.fori_loop(0, chunks, dots, 0)
+    every = to_lanes(accs, 12, flat)
     pulled = []
     for half in range(2):
-        at = [all_lanes(accs[6 * half + j]) for j in range(6)]
+        at = every[6 * half : 6 * half + 6]
         pair = 0.5 * (at[2] + at[3])
         quad = 0.25 * (at[2] + at[3] + (at[4] + at[5] if half == 0 else at[0] + at[1]))
         for k in (2 * half, 2 * half + 1):
@@ -453,24 +595,25 @@
     spread = triples([pulled[k][2] for k in range(4)], m0, m1)
     quad = 0.25 * (pulled[0][3] + pulled[1][3] + pulled[2][3] + pulled[3][3])
     weights = token_weights(probs, m0, m1)
+    factors = []
     for k in range(4):
         half = k // 2
         pair = 0.5 * (pulled[2 * half][1] + pulled[2 * half + 1][1])
-        accs[k] = (pulled[k][0] + pair + spread[k] * (1.0 / 3.0) + quad) * live[k]
-    inside = (lax.broadcasted_iota(jnp.int32, (rows, 128), 0) >= 8) & (
-        lax.broadcasted_iota(jnp.int32, (rows, 128), 0) < 8 + own
-    )
+        factors.append((pulled[k][0] + pair + spread[k] * (1.0 / 3.0) + quad) * live_lane[k])
+    at_row = lax.broadcasted_iota(jnp.int32, (1, flat.shape[0]), 1)
+    inside = (at_row >= 8) & (at_row < 8 + own)
     even = [jnp.where(inside, weight, 0.0) for weight in weights[0]]
     odd = [jnp.where(inside, weight, 0.0) for weight in weights[1]]
     reached = (
-        (down(odd[4]), even[2], odd[0]),
-        (down(odd[5]), even[3], odd[1]),
-        (even[4], odd[2], up(even[0])),
-        (even[5], odd[3], up(even[1])),
+        (behind_lane(odd[4]), even[2], odd[0]),
+        (behind_lane(odd[5]), even[3], odd[1]),
+        (even[4], odd[2], ahead_lane(even[0])),
+        (even[5], odd[3], ahead_lane(even[1])),
     )
     for k in range(4):
         for j in range(3):
-            accs[4 + 3 * k + j] = reached[k][j] * live[k]
+            factors.append(reached[k][j] * live_lane[k])
+    to_rows(factors, lines, accs)
 
     def back(i, _):
         chunk = lane_chunk(i)
@@ -512,16 +655,33 @@
 
     lax.fori_loop(0, chunks, back, 0)
     row = lax.broadcasted_iota(jnp.int32, (TABLE, 4 * rows), 0)
-    embed_grad[...] += nn((ids_row[...] == row).astype(bf16), emb_grad[...])
-
-
-def pool_back(seq, first, ids, ids_row, table, grad_normed, resid, after_grad, total_bytes):
-    _, wide, _ = ids.shape
+    total = nn((ids_row[...] == row).astype(bf16), emb_grad[...])
+    if given:
+        total = total + embed_before[...]
+    embed_grad[...] = total
+    if last:
+        small_grad[6:7, :] = feed_stats[0:1, :]
+        embed_grad[VOCAB : VOCAB + 7, :] = small_grad[0:7, :]
+        turned[...] = embed_grad[...].T.astype(bf16)
+
+
+def pool_back(
+    seq, first, ids, ids_row, table, pulled, from_core, from_x, dq, qkv, resid, after_grad,
+    feed_stats, before, deps, total_bytes,
+):
+    count, wide, _ = ids.shape
     rows = wide // 4
     tokens = 2 * (rows - 16)
+    last = seq == count - 1
     token_spec = pl.BlockSpec((None, tokens, D), lambda i: (seq, 0, 0))
+    table_sum = pl.BlockSpec((TABLE, D), lambda i: (0, 0))
+    small_sum = pl.BlockSpec((8, D), lambda i: (0, 0))
+    sums = [pltpu.VMEM((TABLE, D), f32), pltpu.VMEM((8, D), f32)]
     return pl.pallas_call(
-        partial(pool_back_kernel, rows=rows, total_bytes=total_bytes),
+        partial(
+            pool_back_kernel, rows=rows, total_bytes=total_bytes, given=bool(before), last=last,
+            deps=len(deps),
+        ),
         grid=(1,),
         in_specs=[
             pl.BlockSpec(memory_space=pltpu.SMEM),
@@ -530,28 +690,37 @@
             pl.BlockSpec((D, TABLE), lambda i: (0, 0)),
             token_spec,
             token_spec,
+            pl.BlockSpec((tokens, D), lambda i: (0, 0)),
             token_spec,
-        ],
-        out_specs=[
-            pl.BlockSpec((TABLE, D), lambda i: (0, 0)),
-            pl.BlockSpec((8, D), lambda i: (0, 0)),
-        ],
-        out_shape=[
-            jax.ShapeDtypeStruct((TABLE, D), f32),
-            jax.ShapeDtypeStruct((8, D), f32),
-        ],
+            pl.BlockSpec((D, D), lambda i: (0, 0)),
+            token_spec,
+            token_spec,
+            small_sum,
+        ]
+        + ([table_sum, small_sum] if before else [])
+        + [pl.BlockSpec(memory_space=pl.ANY)] * len(deps),
+        out_specs=pl.BlockSpec((D, TABLE), lambda i: (0, 0)) if last else [table_sum, small_sum],
+        out_shape=jax.ShapeDtypeStruct((D, TABLE), bf16)
+        if last
+        else [jax.ShapeDtypeStruct((TABLE, D), f32), jax.ShapeDtypeStruct((8, D), f32)],
         scratch_shapes=[
             pltpu.VMEM((wide, D), f32),
             pltpu.VMEM((8, D), f32),
             pltpu.VMEM((4, rows, D), f32),
             pltpu.VMEM((16, rows, 128), f32),
+            pltpu.VMEM((2 * 128, 128), f32),
+            pltpu.VMEM((16, 2 * 128), f32),
             pltpu.VMEM((D // 128, tokens, 128), f32),
             pltpu.VMEM((2, rows, D), f32),
             pltpu.VMEM((wide, D), bf16),
-        ],
-        cost_estimate=pl.CostEstimate(flops=8_000_000_000, bytes_accessed=8_000_000, transcendentals=0),
+        ]
+        + (sums if last else []),
+        cost_estimate=pl.CostEstimate(flops=9_000_000_000, bytes_accessed=8_000_000, transcendentals=0),
         name="pool_back",
-    )(first, ids, ids_row, table, grad_normed, resid, after_grad)
+    )(
+        first, ids, ids_row, table, pulled, from_core, from_x, dq, qkv, resid, after_grad,
+        feed_stats, *before, *deps,
+    )
 
 
 def prepare_kernel(
@@ -666,7 +835,7 @@
     return jnp.where((lane // HEAD_DIM) == head, values, jnp.zeros_like(values))
 
 
-def attend_kernel(rank_ref, q, k, v, side, bias, out, norm, kcat, vcat, *, near, blocks):
+def attend_kernel(rank_ref, q, kv, side, bias, out, norm, kcat, vcat, *, near, blocks):
     rank = rank_ref[0]
     pair = pl.program_id(1)
     queries = q.shape[0]
@@ -679,8 +848,8 @@
 
     for step in range(2 * blocks):
         source = pl.ds(row_offset(rank, step, blocks), HALF)
-        kcat[step * HALF : (step + 1) * HALF, :SIDE] = k[source, :]
-        vcat[step * HALF : (step + 1) * HALF, :SIDE] = v[source, :]
+        kcat[step * HALF : (step + 1) * HALF, :SIDE] = kv[source, :SIDE]
+        vcat[step * HALF : (step + 1) * HALF, :SIDE] = kv[source, SIDE:]
 
     lane = lax.broadcasted_iota(jnp.int32, (queries, SIDE), 1)
     halves = []
@@ -714,8 +883,7 @@
         in_specs=[
             pl.BlockSpec(memory_space=pltpu.SMEM),
             pl.BlockSpec((None, queries, SIDE), lambda s, i: (s, 0, i)),
-            pl.BlockSpec((None, keys, SIDE), lambda s, i: (s, 0, i)),
-            pl.BlockSpec((None, keys, SIDE), lambda s, i: (s, 0, i + PAIRS)),
+            pl.BlockSpec((None, keys, 2 * SIDE), lambda s, i: (s, 0, i)),
             pl.BlockSpec((None, keys, SIDE), lambda s, i: (s, 0, 0)),
             pl.BlockSpec((2, queries, near), lambda s, i: (i, 0, 0)),
         ],
@@ -730,17 +898,17 @@
         scratch_shapes=[pltpu.VMEM((keys, 2 * SIDE), bf16)] * 2,
         cost_estimate=pl.CostEstimate(flops=25_000_000_000, bytes_accessed=8_000_000, transcendentals=0),
         name="attend",
-    )(rank, q, kv, kv, side, bias)
+    )(rank, q, kv, side, bias)
 
 
 def attend_back_kernel(
-    rank_ref, q, k, v, side, bias, norm, mixed, grad, *rest, near, blocks, part,
+    rank_ref, q, kv, side, bias, norm, mixed, grad, dq, dkv, dnear, dfar, kcat, vcat, kturn, *,
+    near, blocks, part,
 ):
-    dq, dk, dv, dnear, dfar, kcat, vcat, kturn = rest[-8:]
     rank = rank_ref[0]
-    pair = pl.program_id(0)
+    pair = pl.program_id(1)
     queries = q.shape[0]
-    keys = k.shape[0]
+    keys = kv.shape[0]
 
     @pl.when(pair == 0)
     def _():
@@ -750,8 +918,8 @@
 
     for step in range(2 * blocks):
         source = pl.ds(row_offset(rank, step, blocks), HALF)
-        kcat[step * HALF : (step + 1) * HALF, :SIDE] = k[source, :]
-        vcat[step * HALF : (step + 1) * HALF, :SIDE] = v[source, :]
+        kcat[step * HALF : (step + 1) * HALF, :SIDE] = kv[source, :SIDE]
+        vcat[step * HALF : (step + 1) * HALF, :SIDE] = kv[source, SIDE:]
     kturn[:SIDE, :] = kcat[:, :SIDE].astype(f32).T.astype(bf16)
 
     lane = lax.broadcasted_iota(jnp.int32, (queries, SIDE), 1)
@@ -780,7 +948,9 @@
         for head in range(2):
             logits = nt(kcat[span, :], wide_q[head])
             if base < near:
-                logits = logits + bias[head, span, :].astype(f32)
+                here = min(near, base + part) - base
+                close = logits[:here] + bias[head, base : base + here, :].astype(f32)
+                logits = close if here == part else jnp.concatenate([close, logits[here:]], axis=0)
             probs = jnp.exp(logits)
             pull = nt(vcat[span, :], wide_g[head])
             low = (probs * pull).astype(bf16)
@@ -788,51 +958,48 @@
             key_part += nn(low, queries_of[head])
             sums[head] += nn(kturn[:, span], low)
             if base < near:
-                dnear[head, span, :] = low
+                here = min(near, base + part) - base
+                dnear[head, base : base + here, :] = low[:here]
         for step in range(base // HALF, (base + part) // HALF):
             target = pl.ds(row_offset(rank, step, blocks), HALF)
             inner = slice(step * HALF - base, (step + 1) * HALF - base)
-            dk[target, :] = key_part[inner].astype(bf16)
-            dv[target, :] = value_part[inner].astype(bf16)
+            dkv[target, :SIDE] = key_part[inner].astype(bf16)
+            dkv[target, SIDE:] = value_part[inner].astype(bf16)
     turned = jnp.concatenate([sums[0][:HEAD_DIM], sums[1][HEAD_DIM:SIDE]], axis=0)
     dq[...] = turned.T.astype(bf16)
     for head in range(2):
         dfar[head] = sums[head][SIDE:, :]
 
 
-def attend_back(seq, rank, q, kv, side, bias, norm, mixed, grad, earlier):
+def attend_back(rank, q, kv, side, bias, norm, mixed, grad):
     seqs, queries, _ = q.shape
     keys = kv.shape[1]
     near = bias.shape[1]
     blocks = keys // queries
-    own = pl.BlockSpec((None, queries, SIDE), lambda i: (seq, 0, i))
-    every = pl.BlockSpec((None, keys, SIDE), lambda i: (seq, 0, i))
+    own = pl.BlockSpec((None, queries, SIDE), lambda s, i: (s, 0, i))
+    every = pl.BlockSpec((None, keys, 2 * SIDE), lambda s, i: (s, 0, i))
     return pl.pallas_call(
-        partial(attend_back_kernel, near=near, blocks=blocks, part=2 * HALF),
-        grid=(PAIRS,),
+        partial(attend_back_kernel, near=near, blocks=blocks, part=KEY_PART),
+        grid=(seqs, PAIRS),
         in_specs=[
             pl.BlockSpec(memory_space=pltpu.SMEM),
             own,
             every,
-            pl.BlockSpec((None, keys, SIDE), lambda i: (seq, 0, i + PAIRS)),
-            pl.BlockSpec((None, keys, SIDE), lambda i: (seq, 0, 0)),
-            pl.BlockSpec((2, near, queries), lambda i: (i, 0, 0)),
-            pl.BlockSpec((None, queries, SIDE), lambda i: (seq, 0, 0)),
+            pl.BlockSpec((None, keys, SIDE), lambda s, i: (s, 0, 0)),
+            pl.BlockSpec((2, near, queries), lambda s, i: (i, 0, 0)),
+            pl.BlockSpec((None, queries, SIDE), lambda s, i: (s, 0, 0)),
             own,
             own,
-        ]
-        + [pl.BlockSpec(memory_space=pl.ANY)] * len(earlier),
+        ],
         out_specs=[
             own,
             every,
-            every,
-            pl.BlockSpec((None, 2, near, queries), lambda i: (seq, i, 0, 0)),
-            pl.BlockSpec((None, 2, ONES, queries), lambda i: (seq, i, 0, 0)),
+            pl.BlockSpec((None, 2, near, queries), lambda s, i: (s, i, 0, 0)),
+            pl.BlockSpec((None, 2, ONES, queries), lambda s, i: (s, i, 0, 0)),
         ],
         out_shape=[
             jax.ShapeDtypeStruct((seqs, queries, D), bf16),
-            jax.ShapeDtypeStruct((seqs, keys, D), bf16),
-            jax.ShapeDtypeStruct((seqs, keys, D), bf16),
+            jax.ShapeDtypeStruct((seqs, keys, 2 * D), bf16),
             jax.ShapeDtypeStruct((seqs, HEADS, near, queries), bf16),
             jax.ShapeDtypeStruct((seqs, HEADS, ONES, queries), f32),
         ],
@@ -841,74 +1008,80 @@
             pltpu.VMEM((keys, 2 * SIDE), bf16),
             pltpu.VMEM((SIDE + ONES, keys), bf16),
         ],
-        input_output_aliases={9 + i: i for i in range(len(earlier))},
-        cost_estimate=pl.CostEstimate(flops=15_000_000_000, bytes_accessed=12_000_000, transcendentals=0),
+        cost_estimate=pl.CostEstimate(flops=40_000_000_000, bytes_accessed=12_000_000, transcendentals=0),
         name="attend_back",
-    )(rank, q, kv, kv, side, bias, norm, mixed, grad, *earlier)
-
-
-def bias_grad_kernel(rank_ref, near, far, out, hot, *, parts):
+    )(rank, q, kv, side, bias, norm, mixed, grad)
+
+
+def bias_grad_kernel(rank_ref, near, far, *rest, parts):
+    out, lines = rest[-2:]
     rank = rank_ref[0]
+    head = pl.program_id(0)
     seqs = near.shape[0]
     steps = near.shape[1] // HALF - 2
-
-    @pl.when(pl.program_id(0) == 0)
-    def _():
-        place = lax.broadcasted_iota(jnp.int32, hot.shape, 0)
-        lane = lax.broadcasted_iota(jnp.int32, hot.shape, 1)
-        segment = place // (2 * HALF)
-        relative = (segment - 1) * HALF + HALF - 1 - lax.rem(place, 2 * HALF)
-        bucket = jnp.where(segment == 3, 15, jnp.where(segment == 4, 31, bucket_of(relative)))
-        hot[...] = (bucket == lane).astype(bf16)
-
-    row = lax.broadcasted_iota(jnp.int32, (HALF, HALF), 0)
-    lane = lax.broadcasted_iota(jnp.int32, (HALF, HALF), 1)
-    flip = (row + lane == HALF - 1).astype(bf16)
-    ones = jnp.ones((8, HALF), bf16)
     first_in, last_in = rank != 0, rank != parts - 1
 
-    def block(s, n, q):
-        return near[s, n * HALF : (n + 1) * HALF, q * HALF : (q + 1) * HALF]
+    def block(n, q):
+        rows, cols = slice(n * HALF, (n + 1) * HALF), slice(q * HALF, (q + 1) * HALF)
+        return sum(near[s, rows, cols].astype(f32) for s in range(seqs))
 
     sums = [jnp.zeros((HALF, HALF), f32) for _ in range(3)]
-    left = [far[s, LEFT - ONES : LEFT - ONES + 1, :] for s in range(seqs)]
-    right = [far[s, RIGHT - ONES : RIGHT - ONES + 1, :] for s in range(seqs)]
-    left, right = sum(left), sum(right)
+    left = sum(far[s, LEFT - ONES : LEFT - ONES + 1, :] for s in range(seqs))
+    right = sum(far[s, RIGHT - ONES : RIGHT - ONES + 1, :] for s in range(seqs))
+    left = [left[:, q * HALF : (q + 1) * HALF] for q in range(steps)]
+    right = [right[:, q * HALF : (q + 1) * HALF] for q in range(steps)]
     for n in range(steps + 2):
         inside = first_in if n == 0 else last_in if n == steps + 1 else None
-        tails = []
         for q in range(steps):
+            value = block(n, q)
             apart = n - 1 - q
+            if inside is not None:
+                column = jnp.sum(value, axis=0, keepdims=True)
+                outer = jnp.where(inside, 0.0, column)
+                if n == 0:
+                    right[q] += outer
+                else:
+                    left[q] += outer
+                kept = jnp.where(inside, column, 0.0)
+                if apart < -1:
+                    left[q] += kept
+                elif apart > 1:
+                    right[q] += kept
+                value = jnp.where(inside, value, 0.0)
             if abs(apart) <= 1:
-                value = sum(nn(flip, block(s, n, q)) for s in range(seqs))
-                if inside is not None:
-                    value = jnp.where(inside, value, 0.0)
                 sums[apart + 1] += value
-        if inside is not None:
-            span = slice(n * HALF, (n + 1) * HALF)
-            column = sum(nn(ones, near[s, span, :]) for s in range(seqs))[:1]
-            at = lax.broadcasted_iota(jnp.int32, column.shape, 1) // HALF
-            outside = (n - 1 - at < -1) | (n - 1 - at > 1)
-            kept = jnp.where(outside, column, 0.0)
-            if n == 0:
-                left += jnp.where(inside, kept, 0.0)
-                right += jnp.where(inside, 0.0, column)
-            else:
-                right += jnp.where(inside, kept, 0.0)
-                left += jnp.where(inside, 0.0, column)
-    lines = []
+    found = []
     for value in sums:
         wide = jnp.concatenate([value, jnp.zeros((HALF, HALF), f32)], axis=1)
-        rolled = pltpu.roll(wide, 0, 1, stride=1, stride_axis=0)
-        lines.append(jnp.sum(rolled, axis=0, keepdims=True))
-    line = jnp.concatenate(lines + [left, right], axis=1)
-    line = jnp.broadcast_to(line, (8, line.shape[1]))
-    total = sum(nn(part.astype(bf16), hot[...]) for part in three_parts(line))
-    out[...] = total[:1]
-
-
-def bias_sums(rank, near_parts, far_parts, parts):
+        folded = wide[0:8, :]
+        for a in range(8, HALF, 8):
+            folded += pltpu.roll(wide[a : a + 8, :], 2 * HALF - a, 1)
+        line = folded[0:1, :]
+        for b in range(1, 8):
+            line += pltpu.roll(folded[b : b + 1, :], 2 * HALF - b, 1)
+        found.append(line)
+    found += [jnp.concatenate(left, axis=1), jnp.concatenate(right, axis=1)]
+    lines[pl.ds(head, 1), :] = jnp.concatenate(found, axis=1)
+
+    @pl.when(head == pl.num_programs(0) - 1)
+    def _():
+        shape = (10 * HALF, 128)
+        place = lax.broadcasted_iota(jnp.int32, shape, 0)
+        lane = lax.broadcasted_iota(jnp.int32, shape, 1)
+        segment, inner = place // (2 * HALF), lax.rem(place, 2 * HALF)
+        behind = jnp.where(inner < HALF, inner, inner - 2 * HALF)
+        relative = (segment - 1) * HALF - behind
+        bucket = jnp.where(segment == 3, 15, jnp.where(segment == 4, 31, bucket_of(relative)))
+        hot = (bucket == lane).astype(bf16)
+        split = jnp.concatenate([part.astype(bf16) for part in three_parts(lines[...])], axis=0)
+        total = nn(split, hot)
+        rows = lines.shape[0]
+        out[...] = total[:rows] + total[rows : 2 * rows] + total[2 * rows :]
+
+
+def bias_sums(rank, near_parts, far_parts, parts, deps):
     seqs, heads, near, queries = near_parts.shape
+    assert queries == 2 * HALF
     return pl.pallas_call(
         partial(bias_grad_kernel, parts=parts),
         grid=(heads,),
@@ -916,13 +1089,14 @@
             pl.BlockSpec(memory_space=pltpu.SMEM),
             pl.BlockSpec((seqs, None, near, queries), lambda i: (0, i, 0, 0)),
             pl.BlockSpec((seqs, None, ONES, queries), lambda i: (0, i, 0, 0)),
-        ],
-        out_specs=pl.BlockSpec((None, 1, 128), lambda i: (i, 0, 0)),
-        out_shape=jax.ShapeDtypeStruct((heads, 1, 128), f32),
-        scratch_shapes=[pltpu.VMEM((10 * HALF, 128), bf16)],
+        ]
+        + [pl.BlockSpec(memory_space=pl.ANY)] * len(deps),
+        out_specs=pl.BlockSpec((16, 128), lambda i: (0, 0)),
+        out_shape=jax.ShapeDtypeStruct((16, 128), f32),
+        scratch_shapes=[pltpu.VMEM((16, 10 * HALF), f32)],
         cost_estimate=pl.CostEstimate(flops=6_000_000_000, bytes_accessed=9_000_000, transcendentals=0),
         name="bias_sums",
-    )(rank, near_parts, far_parts)
+    )(rank, near_parts, far_parts, *deps)
 
 
 def gelu_parts(x):
@@ -1063,29 +1237,20 @@
     shard = score_weight.shape[0]
     rank_ref = rank.reshape(1).astype(jnp.int32)
 
-    live_here = jnp.sum(jnp.minimum((lengths + 1) // 2, total_tokens))
-    live_here = jnp.where(rank == 0, live_here, 0)
-    counts = jnp.stack([live_here // 64, live_here % 64])
-    at_count = (jnp.arange(shard) == 0).astype(jnp.int32)
-    columns = jnp.concatenate(
-        [
-            embed_table,
-            conv_weight,
-            score_weight[None],
-            attn_gain[None],
-            ffn_gain[None],
-            (counts[:, None] * at_count[None]).astype(bf16),
-            jnp.zeros((TABLE - VOCAB - 9, shard), bf16),
-        ],
-        axis=0,
-    ).T
+    tiled = down_weight.shape[0] % 64 == 0
+    third = D // 3
+    columns, *attn_halves, packed = (pack if tiled else pack_plain)(
+        rank_ref, lengths, embed_table, conv_weight,
+        (score_weight[None], attn_gain[None], ffn_gain[None]),
+        (query_weight, key_weight, value_weight),
+        (gate_weight, up_weight, down_weight, output_weight), total_tokens,
+    )
     ids_low = jnp.stack([byte_ids // 16, byte_ids % 16]).astype(bf16)
     id_rows = ids_low.reshape(-1, TABLE)
-    attn_rows = jnp.concatenate([query_weight, key_weight, value_weight], axis=1)
-    cut = attn_rows.shape[1] // 2
+    cut = attn_halves[0].shape[1]
     qkv_halves = [
-        RowGather(attn_rows[:, :cut], gather_order("y")),
-        RowGather(attn_rows[:, cut:], gather_order("x")),
+        RowGather(attn_halves[0], gather_order("y")),
+        RowGather(attn_halves[1], gather_order("x")),
     ]
     small = RowGather(columns, axis_bits("dp"))
     while small.order:
@@ -1129,14 +1294,7 @@
     other_ids = phases(first_other)
 
     ffn_dim = gate_weight.shape[1]
-    tiled = down_weight.shape[0] % 64 == 0
-    third = D // 3
-    if tiled:
-        down_packed = down_weight.reshape(-1, 8, 8, 3, third).transpose(0, 3, 2, 1, 4)
-    else:
-        down_packed = down_weight
-    down_packed = down_packed.reshape(shard, ffn_dim)
-    packed = jnp.concatenate([gate_weight, up_weight, down_packed, output_weight], axis=1)
+    ffn_dim = gate_weight.shape[1]
     wide_full = lax.all_gather(packed, both, axis=0, tiled=True)
     down_full = wide_full[:, 2 * ffn_dim : 3 * ffn_dim]
     if tiled:
@@ -1160,11 +1318,8 @@
         each.finish(tile)
         each.start()
         each.finish()
-    qkv_full = jnp.concatenate(
-        [each.result().reshape(D, cut) for each in qkv_halves], axis=1
-    )
+    qkv_full = jnp.concatenate([each.result().reshape(D, cut) for each in qkv_halves], axis=1)
     query_full, kv_full = qkv_full[:, :D], qkv_full[:, D:]
-    key_full, value_full = qkv_full[:, D : 2 * D], qkv_full[:, 2 * D :]
     normed = jnp.concatenate([normed_two, normed_other], axis=1)
     own_rows = normed_own.reshape(-1, D)
     queries = dot(own_rows, query_full).astype(bf16).reshape(seqs, own, D)
@@ -1185,112 +1340,102 @@
     gate_grad = jnp.einsum("td,tf->df", ffn_in, gate_low, preferred_element_type=f32)
     up_grad = jnp.einsum("td,tf->df", ffn_in, up_low, preferred_element_type=f32)
     output_grad = jnp.einsum("td,te->de", att, after_low, preferred_element_type=f32).astype(bf16)
-    down_sum = RowSum(down_grad.astype(bf16)[None], sum_order("z"))
-    gate_sum = RowSum(gate_grad.astype(bf16)[None], sum_order("x"))
-    up_sum = RowSum(up_grad.astype(bf16)[None], sum_order("y"))
-    feed_sums = (down_sum, gate_sum, up_sum)
-    for each in feed_sums:
-        each.start()
-    turn = after_sends(after(attended_grad, output_grad), *feed_sums).reshape(seqs, own, D)
-
-    made = ()
-    for s in range(seqs):
-        made = attend_back(
-            s, rank_ref, queries, pairs_kv, side, turned_tile, norms, attended, turn, made
-        )
-        for each in feed_sums:
-            each.finish(made[4])
-            each.start()
-        if s < seqs - 1:
-            turn = after_sends(turn, *feed_sums)
-    dq, dk, dv, near_parts, far_parts = made
-    dk_rows, dv_rows = dk.reshape(-1, D), dv.reshape(-1, D)
-    dk_rows = after_sends(dk_rows, *feed_sums)
-    pulled = (
-        jnp.einsum("te,de->td", dk_rows, key_full, preferred_element_type=f32)
-        + jnp.einsum("te,de->td", dv_rows, value_full, preferred_element_type=f32)
-    ).reshape(seqs, total_tokens, D)
-    direct = jnp.einsum(
-        "te,de->td", dq.reshape(-1, D), query_full, preferred_element_type=f32
-    ).reshape(seqs, own, D)
-    from_core = swap(pulled[:, 2 * own :].astype(bf16), "seq", 1)
+    down_grad = down_grad.astype(bf16)
+    if tiled:
+        down_grad = down_grad.reshape(-1, 8, 8, 3, third).transpose(0, 3, 2, 1, 4)
+    wide_grad = jnp.concatenate(
+        [
+            gate_grad.astype(bf16),
+            up_grad.astype(bf16),
+            down_grad.reshape(D, ffn_dim),
+            output_grad,
+        ],
+        axis=1,
+    )
+    wide_sum = lax.psum_scatter(wide_grad, both, scatter_dimension=0, tiled=True)
+    turn = after(attended_grad, wide_grad).reshape(seqs, own, D)
+    dq, dkv, near_parts, far_parts = attend_back(
+        rank_ref, queries, pairs_kv, side, turned_tile, norms, attended, turn
+    )
+    dq_rows, dkv_rows = dq.reshape(-1, D), dkv.reshape(-1, 2 * D)
+    pulled = jnp.einsum("te,de->td", dkv_rows, kv_full, preferred_element_type=f32)
+    pulled = pulled.astype(bf16).reshape(seqs, total_tokens, D)
+    to_core = pulled[:, 2 * own :]
+    from_core = swap(to_core, "seq", 1)
+    query_grad = jnp.einsum(
+        "td,te->de", own_rows, after(dq_rows, to_core), preferred_element_type=f32
+    ).astype(bf16)
+    from_core = after(from_core, query_grad)
+    to_x = [
+        (pulled[s, own : 2 * own].astype(f32) + from_core[s, own:].astype(f32)).astype(bf16)
+        for s in range(seqs)
+    ]
+    from_x = [swap(rows, "seq", 2) for rows in to_x]
     normed_rows = normed.reshape(-1, D)
-    key_grad = jnp.einsum(
-        "td,te->de", normed_rows, after(dk_rows, pulled), preferred_element_type=f32
+    kv_grad = jnp.einsum(
+        "td,te->de", normed_rows, after(dkv_rows, *to_x), preferred_element_type=f32
     ).astype(bf16)
-    from_core = after(from_core, key_grad)
-    chip = pulled[:, : 2 * own] + from_core.astype(f32)
-    from_x = swap(chip[:, own:].astype(bf16), "seq", 2)
-    for each in feed_sums:
-        each.finish(key_grad)
-        each.start()
-    dv_rows = after_sends(after(dv_rows, chip), *feed_sums)
-    value_grad = jnp.einsum("td,te->de", normed_rows, dv_rows, preferred_element_type=f32)
-    query_grad = jnp.einsum(
-        "td,te->de", own_rows, after(dq.reshape(-1, D), chip), preferred_element_type=f32
-    )
-    attn_sum = RowSum(
-        jnp.stack([query_grad.astype(bf16), key_grad, value_grad.astype(bf16), output_grad]),
-        sum_order("y"),
-    )
+    attn_sum = RowSum(jnp.concatenate([query_grad, kv_grad], axis=1)[None], sum_order("y"))
     attn_sum.start()
-    bias_rows = bias_sums(rank_ref, after_sends(near_parts, attn_sum), far_parts, parts)
+    bias_rows = bias_sums(rank_ref, near_parts, far_parts, parts, [attn_sum.sent])
     attn_sum.finish(bias_rows)
     attn_sum.start()
-    from_x = after_sends(after(from_x, bias_rows), attn_sum)
-    normed_grad = chip[:, :own] + direct + from_x.astype(f32)
     shared = SumEverywhere(
-        jnp.concatenate(
-            [
-                bias_rows.reshape(HEADS, 128),
-                jnp.broadcast_to(jnp.sum(feed_stats[1]), (16 - HEADS, 128)),
-            ],
-            axis=0,
+        jnp.where(
+            (jnp.arange(16) < HEADS)[:, None],
+            bias_rows,
+            jnp.broadcast_to(jnp.sum(feed_stats[1]), (16, 128)),
         )
     )
     shared.start()
-
-    embed_part, small_part = 0.0, 0.0
+    sums, deps = (), [attn_sum.sent]
     for s in range(seqs):
-        a, b = pool_back(
+        sums = pool_back(
             s, first_byte.reshape(1), phase_ids[:, :, None], phase_ids[:, None, :], table,
-            normed_grad, residual, after_grad.reshape(seqs, own, D), total_bytes,
+            pulled, from_core, from_x[s], dq, qkv_full, residual,
+            after_grad.reshape(seqs, own, D), feed_stats, sums, deps, total_bytes,
         )
-        embed_part, small_part = embed_part + a, small_part + b
-        attn_sum.finish(b)
-        shared.finish(b)
-        attn_sum.start()
-        shared.start()
         if s < seqs - 1:
-            normed_grad = after(after_sends(normed_grad, attn_sum), shared.value)
-    front = jnp.concatenate(
-        [
-            embed_part[:VOCAB],
-            small_part[:6],
-            feed_stats[:1],
-            jnp.zeros((TABLE - VOCAB - 7, D), f32),
-        ],
-        axis=0,
-    )
-    front_sum = RowSum(front.T[None], sum_order("x"))
+            shared.finish(sums[1])
+            shared.start()
+            deps = [shared.value]
+        if s == seqs - 2:
+            attn_sum.finish(sums[1])
+            attn_sum.start()
+            deps.append(attn_sum.sent)
+    shared.finish(sums)
+    shared.start()
+    front_sum = RowSum(sums[None], sum_order("x"))
+    while front_sum.order:
+        front_sum.start()
+        for each in (attn_sum, shared):
+            each.finish()
+            each.start()
+        front_sum.finish()
     front_sum = front_sum.result().reshape(shard, TABLE).T
-    sums = shared.result()
-    bias_grad = sums[:HEADS, :BUCKETS].T
-    attn_sum = attn_sum.result()
-    gate_sum, up_sum, down_sum = [each.result()[0] for each in (gate_sum, up_sum, down_sum)]
+    every = shared.result()
+    bias_grad = every[:HEADS, :BUCKETS].T
+    attn_sum = attn_sum.result()[0]
+    kv_sum = attn_sum[:, D : 3 * D].reshape(shard, PAIRS, 2, SIDE)
+    wide_sum = wide_sum.astype(f32)
+    gate_sum, up_sum = wide_sum[:, :ffn_dim], wide_sum[:, ffn_dim : 2 * ffn_dim]
+    down_sum = wide_sum[:, 2 * ffn_dim : 3 * ffn_dim]
+    if tiled:
+        down_sum = down_sum.reshape(-1, 3, 8, 8, third).transpose(0, 3, 2, 1, 4)
+    down_sum = down_sum.reshape(-1, D)
 
     return (
         block_out.reshape(seqs, own, D),
-        sums[HEADS, 0] / live_count,
+        every[HEADS, 0] / live_count,
         front_sum[:VOCAB],
         front_sum[VOCAB : VOCAB + 4],
         front_sum[VOCAB + 4],
         front_sum[VOCAB + 5],
         bias_grad,
-        attn_sum[0],
-        attn_sum[1],
-        attn_sum[2],
-        attn_sum[3],
+        attn_sum[:, :D],
+        kv_sum[:, :, 0].reshape(shard, D),
+        kv_sum[:, :, 1].reshape(shard, D),
+        wide_sum[:, 3 * ffn_dim :],
         front_sum[VOCAB + 6],
         gate_sum,
         up_sum,

time: 462 us -> 405 us (0.88)
  other arithmetic: 55.3 us -> 32.3 us
  local copies, waits for them, and re-layouts: 53.3 us -> 37.3 us
  Pallas kernels: 182 us -> 172 us
    convert_element_type x15 -> x6, other arithmetic: 20.4 us -> 3.61 us  [start(): self.sent = send.astype(bf16)]
    pallas_call x3 -> x1, Pallas kernels: 49.3 us -> 34.1 us  [attend_back(): pl.pallas_call(partial(attend_back_kernel, near=near, blocks=blocks, part...]
    dynamic_slice x30 -> x12, local copies, waits for them, and re-layouts: 20.3 us -> 5.63 us  [half(): picked = lax.dynamic_index_in_dim(cut, which, 1, keepdims=False)]
    add x4 -> x0, other arithmetic: 7.42 us -> none  [the longest x1 4.35 us: per_device(): chip = pulled[:, :2 * own] + from_core.astype(f32)]
    squeeze x3 -> x1, other arithmetic: 5.37 us -> 0.09 us  [per_device(): attn_sum = attn_sum.result()[0]]
    dot_general x6 -> x3, matrix products: 28.6 us -> 26.5 us  [the longest x1 12.6 us: per_device(): jnp.einsum('td,te->de', normed_rows, after(dkv_rows, *to_x), preferred_el...]
    ppermute x48 -> x35, starting transfers between devices: 41.7 us -> 40.5 us  [swap(): return lax.ppermute(value, axis, [(i, i ^ bit) for i in range(peers)])]
    ppermute x48 -> x35, waiting for transfers between devices: 51.9 us -> 51.5 us  [swap(): return lax.ppermute(value, axis, [(i, i ^ bit) for i in range(peers)])]
  transfers between devices with their start and end apart: 49 -> 37, of which waited for: 17 -> 12; matrix products, arithmetic and copies ran while one was open for 24% -> 20% of each run, Pallas kernels for 33% -> 27%
where the time goes in v1:
time: 405 us; the launch traced here: 402 us
  Pallas kernels  172 us (42%)
  waiting for transfers between devices  51.6 us (13%)
  matrix products  50 us (12%)
  starting transfers between devices  40.5 us (10%)
  local copies, waits for them, and re-layouts  37.3 us (9%)
  other arithmetic  32.3 us (8%)
  between operations  18.3 us (5%)
    ppermute x35, waiting for transfers between devices, swap(): return lax.ppermute(value, axis, [(i, i ^ bit) for i in range(peers)])  51.5 us
    ppermute x35, starting transfers between devices, swap(): return lax.ppermute(value, axis, [(i, i ^ bit) for i in range(peers)])  40.5 us
    pallas_call x3, Pallas kernels, pool_back(): pl.pallas_call(partial(pool_back_kernel, rows=rows, total_bytes=total_byt...  35 us
    pallas_call x1, Pallas kernels, attend_back(): pl.pallas_call(partial(attend_back_kernel, near=near, blocks=blocks, part...  34.1 us
    pallas_call x1, Pallas kernels, feed(): pl.pallas_call(partial(feed_kernel, chunk=512), grid=(seqs,), in_specs=[s...  29.5 us
    pallas_call x1, Pallas kernels, attend(): pl.pallas_call(partial(attend_kernel, near=near, blocks=blocks), grid=(se...  26.8 us
    pallas_call x2, Pallas kernels, pool(): pl.pallas_call(partial(pool_kernel, rows=rows, total_bytes=total_bytes),...  25.9 us
    dot_general x1, matrix products, per_device(): jnp.einsum('td,te->de', normed_rows, after(dkv_rows, *to_x), preferred_el...  12.6 us
  transfers between devices with their start and end apart: 37, of which 12 were waited for; matrix products, arithmetic and copies ran while one was open for 20% of the time, Pallas kernels for 27%

profile of v1, /device:TPU:0, one launch (start us, length us, event | category | flops | bytes accessed | tf_op | source)
XLA Modules:
  0.0 402.3 jit_solution(2660216563198794450)
XLA Ops:
  8.7 2.0 pack.1
  10.7 4.1 %collective-permute-start = (bf16[24,384]{1,0:T(8,128)(2,1)}, bf16[24,384]{1,0:T(8,128)(2,1)S(1)}, u32[]{:S(2)}, u32[]{:S(2)}) collective-permute-start(bf16[24,384]{1,0:T(8,128)(2,1)} %get-tuple-element.60), channel_id=1, source_target_pairs={{0,16},{4,20},{8,24},{12,28},{16,0},{20,4},{24,8},{28,12},{1,17},{... | collective-permute-start | bytes 55304 | tf_op jit(solution)/shard_map/ppermute | solution.py:55
  14.9 2.8 collective-permute-start.11
  31.1 3.4 collective-permute-done.6
  34.5 2.3 collective-permute-done.12
  43.3 13.2 %pool.2 = (f32[3,256,768]{2,1,0:T(8,128)}, bf16[3,256,768]{2,1,0:T(8,128)(2,1)}) custom-call(s32[1]{0:T(128)} %bitcast.19.first_ref, s32[3,576,1]{2,1,0:T(8,128)} %broadcast_in_dim_reshape.18.ids, bf16[768,384]{1,0:T(8,128)(2,1)} %bitcast.235), custom_call_target="tpu_custom_call" | custom-call | flops 8999999488 | bytes 4000000 | tf_op jit(solution)/shard_map/pool/pallas_call | solution.py:487
  62.4 12.7 %pool.3 = (f32[3,256,768]{2,1,0:T(8,128)}, bf16[3,256,768]{2,1,0:T(8,128)(2,1)}) custom-call(s32[1]{0:T(128)} %bitcast.31.first_ref, s32[3,576,1]{2,1,0:T(8,128)} %broadcast_in_dim_reshape.17.ids, bf16[768,384]{1,0:T(8,128)(2,1)} %bitcast.236), custom_call_target="tpu_custom_call" | custom-call | flops 8999999488 | bytes 4000000 | tf_op jit(solution)/shard_map/pool/pallas_call | solution.py:487
  77.6 8.4 %prepare.1 = (bf16[12,256,512]{2,1,0:T(8,128)(2,1)}, bf16[12,512,256]{2,1,0:T(8,128)(2,1)}, bf16[3,1024,128]{2,1,0:T(8,128)(2,1)}) custom-call(s32[1]{0:T(128)} %bitcast.1.rank_ref, s32[3]{0:T(128)} %lengths_ref.5, f32[32,12]{1,0:T(8,128)} %copy.109.bias_ref, bf16[32,128]{1,0:T(8,128)(2,1)} %pad.9.lanes_bias), custom_call_target="tpu_custom_call" | custom-call | flops 6000000000 | bytes 7000000 | tf_op jit(solution)/shard_map/prepare/pallas_call | solution.py:791
  95.3 2.1 convolution_convert_fusion.8
  98.0 9.9 %convolution_convert_fusion = bf16[3072,1536]{1,0:T(8,128)(2,1)} fusion(bf16[3072,768]{1,0:T(8,128)(2,1)S(1)} %bitcast.208, bf16[768,1152]{1,0:T(8,128)(2,1)S(1)} %bitcast.201, bf16[768,1152]{1,0:T(8,128)(2,1)S(1)} %bitcast.197), kind=kOutput, calls=%fused_computation.1 | convolution fusion | flops 7257194496 | bytes 17694720 | tf_op jit(solution)/shard_map/dot_general | solution.py:1210
  107.9 26.8 %attend.1 = (bf16[3,256,768]{2,1,0:T(8,128)(2,1)}, f32[3,256,128]{2,1,0:T(8,128)}) custom-call(s32[1]{0:T(128)} %bitcast.1.rank_ref, bf16[3,256,768]{2,1,0:T(8,128)(2,1)} %bitcast.304, bf16[3,1024,1536]{2,1,0:T(8,128)(2,1)} %bitcast.297, bf16[3,1024,128]{2,1,0:T(8,128)(2,1)} %get-tuple-element.72.side, bf16[12,256,512]{2,1,0:T(8,128)(2,1)} %get-tuple-element.67.bias), custom_call_target="tpu_custom_call" | custom-call | flops 24999999488 | bytes 8000000 | tf_op jit(solution)/shard_map/attend/pallas_call | solution.py:880
  134.6 1.9 slice-done
  136.5 2.0 copy.113
  138.6 29.5 %feed.1 = (f32[768,768]{1,0:T(8,128)}, bf16[768,768]{1,0:T(8,128)(2,1)}, bf16[768,2048]{1,0:T(8,128)(2,1)}, bf16[768,768]{1,0:T(8,128)(2,1)}, bf16[768,2048]{1,0...) custom-call(s32[1]{0:T(128)} %bitcast.place_ref, ...), custom_call_target="tpu_custom_call" | custom-call | flops 16999999488 | bytes 30000000 | tf_op jit(solution)/shard_map/feed/pallas_call | solution.py:1174
  168.1 2.5 convolution_convert_fusion.7
  170.6 2.9 convolution_convert_fusion.4
  173.6 2.9 convolution_convert_fusion.3
  176.5 3.2 convolution_convert_fusion.2
  180.0 4.7 %pad_maximum_fusion = bf16[768,6912]{1,0:T(8,128)(2,1)} fusion(bf16[768,768]{1,0:T(8,128)(2,1)S(1)} %convolution_convert_fusion.7, bf16[768,2048]{1,0:T(8,128)(2,1)S(1)} %bitcast.196, bf16[768,2048]{1,0:T(8,128)(2,1)S(1)} %convolution_convert_fusion.3, bf16[768,2048]{1,0:T(8,128)(2,1)S(1)} %convolution_convert_fusion.4), kind=kLoop, calls=%fused_computation.2 | loop fusion | flops 42467328 | bytes 21233664 | tf_op jit(solution)/shard_map/concatenate | solution.py:1346
  184.7 34.1 %attend_back.1 = (bf16[3,256,768]{2,1,0:T(8,128)(2,1)}, bf16[3,1024,1536]{2,1,0:T(8,128)(2,1)}, bf16[3,12,512,256]{3,2,1,0:T(8,128)(2,1)}, f32[3,12,16,256]{3,2,1,0:T(8,128)}) custom-call(s32[1]{0:T(128)} %bitcast.1.rank_ref, bf16[3,256,768]{2,1,0:T(8,128)(2,1)} %bitcast.305, bf16[3,1024,1536]{2,1,0:T(8,128)(2,1)} %bitcast.298, ...), custom_call_target="tpu_custom_call" | custom-call | flops 40000000000 | bytes 12000000 | tf_op jit(solution)/shard_map/attend_back/pallas_call | solution.py:981
  218.8 10.1 %convolution_convert_fusion.1 = bf16[3072,768]{1,0:T(8,128)(2,1)S(1)} fusion(bf16[3072,1536]{1,0:T(8,128)(2,1)} %bitcast.295, bf16[768,1152]{1,0:T(8,128)(2,1)S(1)} %bitcast.202, bf16[768,1152]{1,0:T(8,128)(2,1)S(1)} %bitcast.198), kind=kOutput, calls=%fused_computation.3 | convolution fusion | flops 7254835200 | bytes 17694720 | tf_op jit(solution)/shard_map/te,de->td/dot_general | solution.py:1361
  233.3 3.8 convolution_convert_fusion.6
  237.1 2.4 copy.116
  239.5 2.9 fusion.4
  242.4 12.6 %convolution_convert_fusion.5 = bf16[768,1536]{1,0:T(8,128)(2,1)S(1)} fusion(bf16[3072,768]{1,0:T(8,128)(2,1)} %bitcast.209, bf16[3072,1536]{1,0:T(8,128)(2,1)} %bitcast.296), kind=kOutput, calls=%fused_computation.12 | convolution fusion | flops 7248936960 | bytes 16515072 | tf_op jit(solution)/shard_map/td,te->de/dot_general | solution.py:1375
  255.2 2.0 constant_dynamic-slice_fusion.12
  257.6 2.0 pad_maximum_fusion.2.query_w
  260.9 2.2 collective-permute-start.23
  263.1 2.0 collective-permute-start.18
  265.1 10.6 %bias_sums.1 = f32[16,128]{1,0:T(8,128)} custom-call(s32[1]{0:T(128)} %bitcast.1.rank_ref, bf16[3,12,512,256]{3,2,1,0:T(8,128)(2,1)} %get-tuple-element.87.near, f32[3,12,16,256]{3,2,1,0:T(8,128)} %get-tuple-element.88.far, bf16[1,384,2304]{2,1,0:T(8,128)(2,1)} %bitcast.70.rest_0_), custom_call_target="tpu_custom_call" | custom-call | flops 6000000000 | bytes 9000000 | tf_op jit(solution)/shard_map/bias_sums/pallas_call | solution.py:1085
  277.3 2.4 add_convert_fusion
  280.5 10.9 %collective-permute-done.18.from_x = bf16[256,768]{1,0:T(8,128)(2,1)} collective-permute-done((bf16[256,768]{1,0:T(8,128)(2,1)}, bf16[256,768]{1,0:T(8,128)(2,1)}, u32[]{:S(2)}, u32[]{:S(2)}) %collective-permute-start.18) | collective-permute-done | bytes 393248 | tf_op jit(solution)/shard_map/ppermute | solution.py:55
  291.4 11.4 %pool_back.3 = (f32[384,768]{1,0:T(8,128)}, f32[8,768]{1,0:T(8,128)}) custom-call(s32[1]{0:T(128)} %bitcast.19.first_ref, s32[3,576,1]{2,1,0:T(8,128)} %broadcast_in_dim_reshape.18.ids, s32[3,1,576]{2,1,0:T(1,128)} %broadcast_in_dim_reshape.16.ids_row, bf16[768,384]{1,0:T(8,128)(2,1)} %bitcast.239, bf16[3,1024,768]{2,1,0:T(8,128)(2,1)} %bitcast.218, ...), custom_call_target="tpu_custom_call" | custom-call | flops 8999999488 | bytes 8000000 | tf_op jit(solution)/shard_map/pool_back/pallas_call | solution.py:680
  304.1 2.5 collective-permute-start.20
  306.6 11.7 %pool_back.4 = (f32[384,768]{1,0:T(8,128)}, f32[8,768]{1,0:T(8,128)}) custom-call(s32[1]{0:T(128)} %bitcast.19.first_ref, s32[3,576,1]{2,1,0:T(8,128)} %broadcast_in_dim_reshape.18.ids, s32[3,1,576]{2,1,0:T(1,128)} %broadcast_in_dim_reshape.16.ids_row, bf16[768,384]{1,0:T(8,128)(2,1)} %bitcast.240, bf16[3,1024,768]{2,1,0:T(8,128)(2,1)} %bitcast.219, ...), custom_call_target="tpu_custom_call" | custom-call | flops 8999999488 | bytes 8000000 | tf_op jit(solution)/shard_map/pool_back/pallas_call | solution.py:680
  322.2 12.0 %pool_back.5 = bf16[768,384]{1,0:T(8,128)(2,1)} custom-call(s32[1]{0:T(128)} %bitcast.19.first_ref, s32[3,576,1]{2,1,0:T(8,128)} %broadcast_in_dim_reshape.18.ids, s32[3,1,576]{2,1,0:T(1,128)} %broadcast_in_dim_reshape.16.ids_row, bf16[768,384]{1,0:T(8,128)(2,1)} %bitcast.241, bf16[3,1024,768]{2,1,0:T(8,128)(2,1)} %bitcast.220, ...), custom_call_target="tpu_custom_call" | custom-call | flops 8999999488 | bytes 8000000 | tf_op jit(solution)/shard_map/pool_back/pallas_call | solution.py:680
  337.8 3.1 collective-permute-done.25
  340.9 3.9 collective-permute-start.26
  344.8 1.9 collective-permute-done.26
  346.7 2.2 collective-permute-start.28
  349.0 7.9 %collective-permute-done.28 = bf16[1,192,384]{2,1,0:T(8,128)(2,1)S(1)} collective-permute-done((bf16[1,192,384]{2,1,0:T(8,128)(2,1)S(1)}, bf16[1,192,384]{2,1,0:T(8,128)(2,1)S(1)}, u32[]{:S(2)}, u32[]{:S(2)}) %collective-permute-start.28) | collective-permute-done | bytes 147488 | tf_op jit(solution)/shard_map/ppermute | solution.py:55
  356.9 2.3 collective-permute-start.29
  359.3 2.3 collective-permute-done.29
  363.8 1.9 collective-permute-done.30
  365.7 3.7 collective-permute-start.31
  372.1 9.3 %collective-permute-done.33 = bf16[1,48,2304]{2,1,0:T(8,128)(2,1)S(1)} collective-permute-done((bf16[1,48,2304]{2,1,0:T(8,128)(2,1)S(1)}, bf16[1,48,2304]{2,1,0:T(8,128)(2,1)S(1)}, u32[]{:S(2)}, u32[]{:S(2)}) %collective-permute-start.33) | collective-permute-done | bytes 221216 | tf_op jit(solution)/shard_map/ppermute | solution.py:55
  382.3 5.5 %collective-permute-done.34 = bf16[1,24,2304]{2,1,0:T(8,128)(2,1)S(1)} collective-permute-done((bf16[1,24,2304]{2,1,0:T(8,128)(2,1)S(1)}, bf16[1,24,2304]{2,1,0:T(8,128)(2,1)S(1)}, u32[]{:S(2)}, u32[]{:S(2)}) %collective-permute-start.34) | collective-permute-done | bytes 110624 | tf_op jit(solution)/shard_map/ppermute | solution.py:55
  390.3 1.8 fusion.21
  (224 shorter events, 65.3 us)
Async XLA Ops:
  7.2 127.4 %all-gather.2.cloned.1.call-start = ((), (), s32[]{:S(2)}) async-start(), calls=%async_computation.1 | async-start | bytes 10948608 | tf_op jit(solution)/shard_map/all_gather | solution.py:1298
  10.7 379.6 %reduce-scatter.2.cloned.1.call-start = ((), (), s32[]{:S(2)}) async-start(), calls=%async_computation.2 | async-start | bytes 10948608 | tf_op jit(solution)/shard_map/reduce_scatter | solution.py:1355
  10.7 7.8 %collective-permute-start = (bf16[24,384]{1,0:T(8,128)(2,1)}, bf16[24,384]{1,0:T(8,128)(2,1)S(1)}, u32[]{:S(2)}, u32[]{:S(2)}) collective-permute-start(bf16[24,384]{1,0:T(8,128)(2,1)} %get-tuple-element.60), channel_id=1, source_target_pairs={{0,16},{4,20},{8,24},{12,28},{16,0},{20,4},{24,8},{28,12},{1,17},{... | collective-permute-start | bytes 55304 | tf_op jit(solution)/shard_map/ppermute | solution.py:55
  14.8 10.7 %collective-permute-start.5 = (bf16[24,1152]{1,0:T(8,128)(2,1)}, bf16[24,1152]{1,0:T(8,128)(2,1)S(1)}, u32[]{:S(2)}, u32[]{:S(2)}) collective-permute-start(bf16[24,1152]{1,0:T(8,128)(2,1)} %get-tuple-element.62), channel_id=1, source_target_pairs={{0,16},{4,20},{8,24},{12,28},{16,0},{20,4},{24,8},{28,12},{1,17},{... | collective-permute-start | bytes 165896 | tf_op jit(solution)/shard_map/ppermute | solution.py:55
  14.9 12.6 %collective-permute-start.11 = (bf16[24,1152]{1,0:T(8,128)(2,1)}, bf16[24,1152]{1,0:T(8,128)(2,1)S(1)}, u32[]{:S(2)}, u32[]{:S(2)}) collective-permute-start(bf16[24,1152]{1,0:T(8,128)(2,1)} %get-tuple-element.69), channel_id=1, source_target_pairs={{0,16},{4,20},{8,24},{12,28},{16,0},{20,4},{24,8},{28,12},{1,17},{... | collective-permute-start | bytes 165896 | tf_op jit(solution)/shard_map/ppermute | solution.py:55
  19.3 4.6 %collective-permute-start.1 = (bf16[2,24,384]{2,1,0:T(8,128)(2,1)S(1)}, bf16[2,24,384]{2,1,0:T(8,128)(2,1)S(1)}, u32[]{:S(2)}, u32[]{:S(2)}) collective-permute-start(bf16[2,24,384]{2,1,0:T(8,128)(2,1)S(1)} %pad_maximum_fusion.20), channel_id=1, source_target_pairs={{0,8},{4,12},{8,0},{12,4},{16,24},{20,28},{24,16},{28,20},{1,9},{5... | collective-permute-start | bytes 110600 | tf_op jit(solution)/shard_map/ppermute | solution.py:55
  23.9 5.5 %collective-permute-start.2 = (bf16[2,2,24,384]{3,2,0,1:T(8,128)(2,1)S(1)}, bf16[2,2,24,384]{3,2,0,1:T(8,128)(2,1)S(1)}, u32[]{:S(2)}, u32[]{:S(2)}) collective-permute-start(bf16[2,2,24,384]{3,2,0,1:T(8,128)(2,1)S(1)} %pad_maximum_fusion.19), channel_id=1, source_target_pairs={{0,4},{4,0},{8,12},{12,8},{16,20},{20,16},{24,28},{28,24},{1,5},{5... | collective-permute-start | bytes 221192 | tf_op jit(solution)/shard_map/ppermute | solution.py:55
  26.4 8.1 %collective-permute-start.6 = (bf16[2,24,1152]{2,1,0:T(8,128)(2,1)S(1)}, bf16[2,24,1152]{2,1,0:T(8,128)(2,1)S(1)}, u32[]{:S(2)}, u32[]{:S(2)}) collective-permute-start(bf16[2,24,1152]{2,1,0:T(8,128)(2,1)S(1)} %pad_maximum_fusion.17), channel_id=1, source_target_pairs={{0,8},{4,12},{8,0},{12,4},{16,24},{20,28},{24,16},{28,20},{1,9},{5... | collective-permute-start | bytes 331784 | tf_op jit(solution)/shard_map/ppermute | solution.py:55
  28.3 8.5 %collective-permute-start.12 = (bf16[2,24,1152]{2,1,0:T(8,128)(2,1)S(1)}, bf16[2,24,1152]{2,1,0:T(8,128)(2,1)S(1)}, u32[]{:S(2)}, u32[]{:S(2)}) collective-permute-start(bf16[2,24,1152]{2,1,0:T(8,128)(2,1)S(1)} %pad_maximum_fusion.18), channel_id=1, source_target_pairs={{0,8},{4,12},{8,0},{12,4},{16,24},{20,28},{24,16},{28,20},{1,9},{5... | collective-permute-start | bytes 331784 | tf_op jit(solution)/shard_map/ppermute | solution.py:55
  29.5 7.4 %collective-permute-start.3 = (bf16[200,384]{1,0:T(8,128)(2,1)S(1)}, bf16[200,384]{1,0:T(8,128)(2,1)S(1)}, u32[]{:S(2)}, u32[]{:S(2)}) collective-permute-start(bf16[200,384]{1,0:T(8,128)(2,1)S(1)} %pad_maximum_fusion.15), channel_id=1, source_target_pairs={{0,2},{1,3},{2,0},{3,1},{4,6},{5,7},{6,4},{7,5},{8,10},{9,11},{10,... | collective-permute-start | bytes 460808 | tf_op jit(solution)/shard_map/ppermute | solution.py:55
  36.9 2.7 collective-permute-start.4
  37.0 21.1 %collective-permute-start.7 = (bf16[2,2,24,1152]{3,2,0,1:T(8,128)(2,1)S(1)}, bf16[2,2,24,1152]{3,2,0,1:T(8,128)(2,1)S(1)}, u32[]{:S(2)}, u32[]{:S(2)}) collective-permute-start(bf16[2,2,24,1152]{3,2,0,1:T(8,128)(2,1)S(1)} %pad_maximum_fusion.13), channel_id=1, source_target_pairs={{0,4},{4,0},{8,12},{12,8},{16,20},{20,16},{24,28},{28,24},{1,5},{5... | collective-permute-start | bytes 663560 | tf_op jit(solution)/shard_map/ppermute | solution.py:55
  38.1 20.1 %collective-permute-start.13 = (bf16[2,2,24,1152]{3,2,0,1:T(8,128)(2,1)S(1)}, bf16[2,2,24,1152]{3,2,0,1:T(8,128)(2,1)S(1)}, u32[]{:S(2)}, u32[]{:S(2)}) collective-permute-start(bf16[2,2,24,1152]{3,2,0,1:T(8,128)(2,1)S(1)} %pad_maximum_fusion.14), channel_id=1, source_target_pairs={{0,2},{1,3},{2,0},{3,1},{4,6},{5,7},{6,4},{7,5},{8,10},{9,11},{10,... | collective-permute-start | bytes 663560 | tf_op jit(solution)/shard_map/ppermute | solution.py:55
  42.0 14.5 %copy-start.19 = (s32[3,4,144]{2,1,0:T(4,128)}, s32[3,4,144]{2,1,0:T(4,128)S(1)}, u32[]{:S(2)}) copy-start(s32[3,4,144]{2,1,0:T(4,128)S(1)} %copy.104) | copy-start | bytes 20740
  59.2 26.9 %collective-permute-start.14 = (bf16[2,2,2,24,1152]{4,3,0,1,2:T(8,128)(2,1)}, bf16[2,2,2,24,1152]{4,3,0,1,2:T(8,128)(2,1)}, u32[]{:S(2)}, u32[]{:S(2)}) collective-permute-start(bf16[2,2,2,24,1152]{4,3,0,1,2:T(8,128)(2,1)} %pad_maximum_fusion.11), channel_id=1, source_target_pairs={{0,4},{4,0},{8,12},{12,8},{16,20},{20,16},{24,28},{28,24},{1,5},{5... | collective-permute-start | bytes 1327112 | tf_op jit(solution)/shard_map/ppermute | solution.py:55
  61.9 14.3 %copy-start.5 = (bf16[3,256,768]{2,1,0:T(8,128)(2,1)S(1)}, bf16[3,256,768]{2,1,0:T(8,128)(2,1)}, u32[]{:S(2)}) copy-start(bf16[3,256,768]{2,1,0:T(8,128)(2,1)} %get-tuple-element.61) | copy-start | bytes 3538948
  61.9 27.4 %collective-permute-start.8 = (bf16[2,2,2,24,1152]{4,3,0,1,2:T(8,128)(2,1)}, bf16[2,2,2,24,1152]{4,3,0,1,2:T(8,128)(2,1)}, u32[]{:S(2)}, u32[]{:S(2)}) collective-permute-start(bf16[2,2,2,24,1152]{4,3,0,1,2:T(8,128)(2,1)} %pad_maximum_fusion.10), channel_id=1, source_target_pairs={{0,2},{1,3},{2,0},{3,1},{4,6},{5,7},{6,4},{7,5},{8,10},{9,11},{10,... | collective-permute-start | bytes 1327112 | tf_op jit(solution)/shard_map/ppermute | solution.py:55
  87.5 5.6 %collective-permute-start.15 = (bf16[2,2,2,2,24,1152]{5,4,0,1,3,2:T(8,128)(2,1)S(1)}, bf16[2,2,2,2,24,1152]{5,4,0,1,3,2:T(8,128)(2,1)S(1)}, u32[]{:S(2)}, u32[]{:S(2)}) collective-permute-start(bf16[2,2,2,2,24,1152]{5,4,0,1,3,2:T(8,128)(2,1)S(1)} %pad_maximum_fusion.8), channel_id=1, source_target_pairs={{0,1},{1,0},{2,3},{3,2},{4,5},{5,4},{6,7},{7,6},{8,9},{9,8},{10,11... | collective-permute-start | bytes 2654216 | tf_op jit(solution)/shard_map/ppermute | solution.py:55
  88.7 8.7 %collective-permute-start.10 = (bf16[3,512,768]{2,1,0:T(8,128)(2,1)S(1)}, bf16[3,512,768]{2,1,0:T(8,128)(2,1)S(1)}, u32[]{:S(2)}, u32[]{:S(2)}) collective-permute-start(bf16[3,512,768]{2,1,0:T(8,128)(2,1)S(1)} %pad_maximum_fusion.4), channel_id=1, source_target_pairs={{0,1},{1,0},{2,3},{3,2},{4,5},{5,4},{6,7},{7,6},{8,9},{9,8},{10,11... | collective-permute-start | bytes 7077896 | tf_op jit(solution)/shard_map/ppermute | solution.py:55
  90.5 4.3 %collective-permute-start.9 = (bf16[2,2,2,2,24,1152]{5,4,0,1,3,2:T(8,128)(2,1)S(1)}, bf16[2,2,2,2,24,1152]{5,4,0,1,3,2:T(8,128)(2,1)S(1)}, u32[]{:S(2)}, u32[]{:S(2)}) collective-permute-start(bf16[2,2,2,2,24,1152]{5,4,0,1,3,2:T(8,128)(2,1)S(1)} %pad_maximum_fusion.7), channel_id=1, source_target_pairs={{0,1},{1,0},{2,3},{3,2},{4,5},{5,4},{6,7},{7,6},{8,9},{9,8},{10,11... | collective-permute-start | bytes 2654216 | tf_op jit(solution)/shard_map/ppermute | solution.py:55
  138.6 29.5 %copy-start.24 = (bf16[3,256,768]{2,1,0:T(8,128)(2,1)S(1)}, bf16[3,256,768]{2,1,0:T(8,128)(2,1)}, u32[]{:S(2)}) copy-start(bf16[3,256,768]{2,1,0:T(8,128)(2,1)} %get-tuple-element.73.mixed) | copy-start | bytes 3538948
  184.7 34.1 %copy-start.1 = (bf16[2,2,2,2,2,24,1152]{6,5,4,3,2,1,0:T(8,128)(2,1)S(1)}, bf16[2,2,2,2,2,24,1152]{6,5,4,3,2,1,0:T(8,128)(2,1)}, u32[]{:S(2)}) copy-start(bf16[2,2,2,2,2,24,1152]{6,5,4,3,2,1,0:T(8,128)(2,1)} %copy-done) | copy-start | bytes 5308420
  184.7 34.1 %copy-start.3 = (bf16[2,2,2,2,2,24,1152]{6,5,4,3,2,1,0:T(8,128)(2,1)S(1)}, bf16[2,2,2,2,2,24,1152]{6,5,4,3,2,1,0:T(8,128)(2,1)}, u32[]{:S(2)}) copy-start(bf16[2,2,2,2,2,24,1152]{6,5,4,3,2,1,0:T(8,128)(2,1)} %copy-done.2) | copy-start | bytes 5308420
  231.9 7.6 %collective-permute-start.16 = (bf16[3,512,768]{2,1,0:T(8,128)(2,1)}, bf16[3,512,768]{2,1,0:T(8,128)(2,1)}, u32[]{:S(2)}, u32[]{:S(2)}) collective-permute-start(bf16[3,512,768]{2,1,0:T(8,128)(2,1)} %slice.148), channel_id=1, source_target_pairs={{0,1},{1,0},{2,3},{3,2},{4,5},{5,4},{6,7},{7,6},{8,9},{9,8},{10,11... | collective-permute-start | bytes 7077896 | tf_op jit(solution)/shard_map/ppermute | solution.py:55
  242.4 12.6 %copy-start.7 = (bf16[768,768]{1,0:T(8,128)(2,1)S(1)}, bf16[768,768]{1,0:T(8,128)(2,1)}, u32[]{:S(2)}) copy-start(bf16[768,768]{1,0:T(8,128)(2,1)} %copy.116) | copy-start | bytes 3538948
  257.3 20.0 %collective-permute-start.19 = (bf16[1,384,2304]{2,1,0:T(8,128)(2,1)}, bf16[1,384,2304]{2,1,0:T(8,128)(2,1)}, u32[]{:S(2)}, u32[]{:S(2)}) collective-permute-start(bf16[1,384,2304]{2,1,0:T(8,128)(2,1)} %bitcast.70.rest_0_), channel_id=1, source_target_pairs={{0,1},{1,0},{2,3},{3,2},{4,5},{5,4},{6,7},{7,6},{8,9},{9,8},{10,11... | collective-permute-start | bytes 5308424 | tf_op jit(solution)/shard_map/ppermute | solution.py:55
  260.9 60.5 %collective-permute-start.23 = (bf16[256,768]{1,0:T(8,128)(2,1)}, bf16[256,768]{1,0:T(8,128)(2,1)S(1)}, u32[]{:S(2)}, u32[]{:S(2)}) collective-permute-start(bf16[256,768]{1,0:T(8,128)(2,1)} %get-tuple-element.170), channel_id=1, source_target_pairs={{0,2},{1,3},{2,0},{3,1},{4,6},{5,7},{6,4},{7,5},{8,10},{9,11},{10,... | collective-permute-start | bytes 1179656 | tf_op jit(solution)/shard_map/ppermute | solution.py:55
  263.1 43.5 %collective-permute-start.21 = (bf16[256,768]{1,0:T(8,128)(2,1)}, bf16[256,768]{1,0:T(8,128)(2,1)}, u32[]{:S(2)}, u32[]{:S(2)}) collective-permute-start(bf16[256,768]{1,0:T(8,128)(2,1)} %get-tuple-element.171), channel_id=1, source_target_pairs={{0,2},{1,3},{2,0},{3,1},{4,6},{5,7},{6,4},{7,5},{8,10},{9,11},{10,... | collective-permute-start | bytes 1179656 | tf_op jit(solution)/shard_map/ppermute | solution.py:55
  263.1 28.3 %collective-permute-start.18 = (bf16[256,768]{1,0:T(8,128)(2,1)}, bf16[256,768]{1,0:T(8,128)(2,1)}, u32[]{:S(2)}, u32[]{:S(2)}) collective-permute-start(bf16[256,768]{1,0:T(8,128)(2,1)} %get-tuple-element.172), channel_id=1, source_target_pairs={{0,2},{1,3},{2,0},{3,1},{4,6},{5,7},{6,4},{7,5},{8,10},{9,11},{10,... | collective-permute-start | bytes 1179656 | tf_op jit(solution)/shard_map/ppermute | solution.py:55
  265.1 12.0 %copy-start.4 = (bf16[16,1,24,2304]{3,2,1,0:T(8,128)(2,1)S(1)}, bf16[16,1,24,2304]{3,2,1,0:T(8,128)(2,1)}, u32[]{:S(2)}) copy-start(bf16[16,1,24,2304]{3,2,1,0:T(8,128)(2,1)} %get-tuple-element.173) | copy-start | bytes 5308420
  277.2 25.6 %collective-permute-start.17 = (f32[16,128]{1,0:T(8,128)S(1)}, f32[16,128]{1,0:T(8,128)S(1)}, u32[]{:S(2)}, u32[]{:S(2)}) collective-permute-start(f32[16,128]{1,0:T(8,128)S(1)} %broadcast_select_fusion.1), channel_id=1, source_target_pairs={{0,1},{1,0},{2,3},{3,2},{4,5},{5,4},{6,7},{7,6},{8,9},{9,8},{10,11... | collective-permute-start | bytes 24584 | tf_op jit(solution)/shard_map/ppermute | solution.py:55
  279.7 40.6 %collective-permute-start.24 = (bf16[1,192,2304]{2,1,0:T(8,128)(2,1)}, bf16[1,192,2304]{2,1,0:T(8,128)(2,1)S(1)}, u32[]{:S(2)}, u32[]{:S(2)}) collective-permute-start(bf16[1,192,2304]{2,1,0:T(8,128)(2,1)} %bitcast.74.rest_0_), channel_id=1, source_target_pairs={{0,4},{4,0},{8,12},{12,8},{16,20},{20,16},{24,28},{28,24},{1,5},{5... | collective-permute-start | bytes 2654216 | tf_op jit(solution)/shard_map/ppermute | solution.py:55
  291.4 11.4 %copy-start.22 = (f32[16,128]{1,0:T(8,128)S(1)}, f32[16,128]{1,0:T(8,128)}, u32[]{:S(2)}) copy-start(f32[16,128]{1,0:T(8,128)} %bias_sums.1) | copy-start | bytes 24580
  304.1 15.4 %collective-permute-start.20 = (f32[16,128]{1,0:T(8,128)}, f32[16,128]{1,0:T(8,128)S(1)}, u32[]{:S(2)}, u32[]{:S(2)}) collective-permute-start(f32[16,128]{1,0:T(8,128)} %fusion.38.rest_2_), channel_id=1, source_target_pairs={{0,2},{1,3},{2,0},{3,1},{4,6},{5,7},{6,4},{7,5},{8,10},{9,11},{10,... | collective-permute-start | bytes 24584 | tf_op jit(solution)/shard_map/ppermute | solution.py:55
  320.3 16.2 %collective-permute-start.22 = (f32[16,128]{1,0:T(8,128)S(1)}, f32[16,128]{1,0:T(8,128)S(1)}, u32[]{:S(2)}, u32[]{:S(2)}) collective-permute-start(f32[16,128]{1,0:T(8,128)S(1)} %add.687.rest_2_), channel_id=1, source_target_pairs={{0,4},{4,0},{8,12},{12,8},{16,20},{20,16},{24,28},{28,24},{1,5},{5... | collective-permute-start | bytes 24584 | tf_op jit(solution)/shard_map/ppermute | solution.py:55
  320.3 13.8 %copy-start.16 = (bf16[1,192,2304]{2,1,0:T(8,128)(2,1)}, bf16[1,192,2304]{2,1,0:T(8,128)(2,1)S(1)}, u32[]{:S(2)}) copy-start(bf16[1,192,2304]{2,1,0:T(8,128)(2,1)S(1)} %collective-permute-done.24) | copy-start | bytes 2654212
  322.2 14.2 %copy-start.17 = (bf16[4,1,24,2304]{3,2,1,0:T(8,128)(2,1)S(1)}, bf16[4,1,24,2304]{3,2,1,0:T(8,128)(2,1)}, u32[]{:S(2)}) copy-start(bf16[4,1,24,2304]{3,2,1,0:T(8,128)(2,1)} %add_convert_fusion.1) | copy-start | bytes 1327108
  335.2 11.4 %collective-permute-start.27 = (bf16[1,384,384]{2,1,0:T(8,128)(2,1)S(1)}, bf16[1,384,384]{2,1,0:T(8,128)(2,1)S(1)}, u32[]{:S(2)}, u32[]{:S(2)}) collective-permute-start(bf16[1,384,384]{2,1,0:T(8,128)(2,1)S(1)} %bitcast.272), channel_id=1, source_target_pairs={{0,1},{1,0},{2,3},{3,2},{4,5},{5,4},{6,7},{7,6},{8,9},{9,8},{10,11... | collective-permute-start | bytes 884744 | tf_op jit(solution)/shard_map/ppermute | solution.py:55
  336.4 33.0 %collective-permute-start.32 = (bf16[1,96,2304]{2,1,0:T(8,128)(2,1)S(1)}, bf16[1,96,2304]{2,1,0:T(8,128)(2,1)S(1)}, u32[]{:S(2)}, u32[]{:S(2)}) collective-permute-start(bf16[1,96,2304]{2,1,0:T(8,128)(2,1)S(1)} %bitcast.255), channel_id=1, source_target_pairs={{0,2},{1,3},{2,0},{3,1},{4,6},{5,7},{6,4},{7,5},{8,10},{9,11},{10,... | collective-permute-start | bytes 1327112 | tf_op jit(solution)/shard_map/ppermute | solution.py:55
  337.2 3.7 collective-permute-start.25
  340.9 5.8 %collective-permute-start.26 = (f32[16,128]{1,0:T(8,128)S(1)}, f32[16,128]{1,0:T(8,128)S(1)}, u32[]{:S(2)}, u32[]{:S(2)}) collective-permute-start(f32[16,128]{1,0:T(8,128)S(1)} %add.693), channel_id=1, source_target_pairs={{0,16},{4,20},{8,24},{12,28},{16,0},{20,4},{24,8},{28,12},{1,17},{... | collective-permute-start | bytes 24584 | tf_op jit(solution)/shard_map/ppermute | solution.py:55
  346.7 10.2 %collective-permute-start.28 = (bf16[1,192,384]{2,1,0:T(8,128)(2,1)S(1)}, bf16[1,192,384]{2,1,0:T(8,128)(2,1)S(1)}, u32[]{:S(2)}, u32[]{:S(2)}) collective-permute-start(bf16[1,192,384]{2,1,0:T(8,128)(2,1)S(1)} %bitcast.280), channel_id=1, source_target_pairs={{0,2},{1,3},{2,0},{3,1},{4,6},{5,7},{6,4},{7,5},{8,10},{9,11},{10,... | collective-permute-start | bytes 442376 | tf_op jit(solution)/shard_map/ppermute | solution.py:55
  356.9 4.7 %collective-permute-start.29 = (bf16[1,96,384]{2,1,0:T(8,128)(2,1)S(1)}, bf16[1,96,384]{2,1,0:T(8,128)(2,1)S(1)}, u32[]{:S(2)}, u32[]{:S(2)}) collective-permute-start(bf16[1,96,384]{2,1,0:T(8,128)(2,1)S(1)} %bitcast.287), channel_id=1, source_target_pairs={{0,4},{4,0},{8,12},{12,8},{16,20},{20,16},{24,28},{28,24},{1,5},{5... | collective-permute-start | bytes 221192 | tf_op jit(solution)/shard_map/ppermute | solution.py:55
  361.6 4.0 %collective-permute-start.30 = (bf16[1,48,384]{2,1,0:T(8,128)(2,1)S(1)}, bf16[1,48,384]{2,1,0:T(8,128)(2,1)S(1)}, u32[]{:S(2)}, u32[]{:S(2)}) collective-permute-start(bf16[1,48,384]{2,1,0:T(8,128)(2,1)S(1)} %bitcast.290), channel_id=1, source_target_pairs={{0,8},{4,12},{8,0},{12,4},{16,24},{20,28},{24,16},{28,20},{1,9},{5... | collective-permute-start | bytes 110600 | tf_op jit(solution)/shard_map/ppermute | solution.py:55
  365.7 5.6 %collective-permute-start.31 = (bf16[1,24,384]{2,1,0:T(8,128)(2,1)S(1)}, bf16[1,24,384]{2,1,0:T(8,128)(2,1)S(1)}, u32[]{:S(2)}, u32[]{:S(2)}) collective-permute-start(bf16[1,24,384]{2,1,0:T(8,128)(2,1)S(1)} %fusion.8), channel_id=1, source_target_pairs={{0,16},{4,20},{8,24},{12,28},{16,0},{20,4},{24,8},{28,12},{1,17},{... | collective-permute-start | bytes 55304 | tf_op jit(solution)/shard_map/ppermute | solution.py:55
  369.5 11.9 %collective-permute-start.33 = (bf16[1,48,2304]{2,1,0:T(8,128)(2,1)S(1)}, bf16[1,48,2304]{2,1,0:T(8,128)(2,1)S(1)}, u32[]{:S(2)}, u32[]{:S(2)}) collective-permute-start(bf16[1,48,2304]{2,1,0:T(8,128)(2,1)S(1)} %bitcast.275), channel_id=1, source_target_pairs={{0,8},{4,12},{8,0},{12,4},{16,24},{20,28},{24,16},{28,20},{1,9},{5... | collective-permute-start | bytes 663560 | tf_op jit(solution)/shard_map/ppermute | solution.py:55
  371.3 22.8 %copy-start.18 = (f32[384,24]{0,1:T(8,128)}, f32[384,24]{0,1:T(8,128)S(1)}, u32[]{:S(2)}) copy-start(f32[384,24]{0,1:T(8,128)S(1)} %fusion.7) | copy-start | bytes 110596
  381.4 6.3 %collective-permute-start.34 = (bf16[1,24,2304]{2,1,0:T(8,128)(2,1)S(1)}, bf16[1,24,2304]{2,1,0:T(8,128)(2,1)S(1)}, u32[]{:S(2)}, u32[]{:S(2)}) collective-permute-start(bf16[1,24,2304]{2,1,0:T(8,128)(2,1)S(1)} %fusion.6), channel_id=1, source_target_pairs={{0,16},{4,20},{8,24},{12,28},{16,0},{20,4},{24,8},{28,12},{1,17},{... | collective-permute-start | bytes 331784 | tf_op jit(solution)/shard_map/ppermute | solution.py:55
  (20 other events, 50.8 us)
Sparse Core Ops, SparseCore 0:
  10.9 97.3 all-gather.1
  232.3 151.8 reduce-scatter.1
